TPU v7x, 32 devices: a whole 2x2x4 slice. The times are simulated.
32 devices in a mesh: row: 4 (over z), col: 8 (over y, x, core).
Axes of the slice: x: 2, y: 2, z: 4, core: 2. Of those that a mesh axis runs over, the one named last changes fastest.
Arguments:
- amplitudes: bfloat16 [2048, 8192], P(('col', 'row')), may hold values from -6 to 6
- integrals: bfloat16 [8192, 8192], P('row', 'col'), may hold values from -0.0625 to 0.0625
- integral_tiles: int32 [64, 64], P('row', 'col'), may hold values from 0 to 1, as said below
- amplitude_tiles: int32 [16, 64], P('col'), may hold values 0 or 1
Outputs:
- ladder: float32 [2048, 8192], P('col', 'row')
Inputs may be any that keep to these rules, and one draw needn't show every extreme that they name: `integral_tiles`: tiles of higher ab index are more often nonzero.
All inputs are finite; a program needn't handle non-finite values. No bound on the sum of `amplitude_tiles` on one device may be relied on, other than what follows from the above.
Results may differ from a plain program's by a relative error of at most 0.0003.
Values may be sent and summed in bfloat16 or wider, within the bound.
No kernel may reach another device: no remote copies, remote signals or barrier semaphores. Data moves between devices by JAX's collectives and lax.ppermute only.
A program may use at most 128 MiB of HBM per device.

v0:
```python
import jax
import jax.numpy as jnp
from jax import lax
from jax.sharding import PartitionSpec as P

TILE = 128


def contract(left, right):
    return lax.dot_general(
        left, right, (((1,), (1,)), ((), ())), preferred_element_type=jnp.float32
    )


def on_device(amplitudes, integrals, integral_tiles, amplitude_tiles):
    local_rows = amplitudes.shape[0]
    tile_rows = jnp.repeat(amplitude_tiles, TILE, axis=0)
    tile_rows = lax.dynamic_slice_in_dim(
        tile_rows, lax.axis_index("row") * local_rows, local_rows, 0
    )
    amp_mask = jnp.repeat(tile_rows, TILE, axis=1).astype(jnp.bfloat16)
    masked_amps = amplitudes * amp_mask
    int_mask = jnp.repeat(jnp.repeat(integral_tiles, TILE, axis=0), TILE, axis=1).astype(
        jnp.bfloat16
    )
    masked_ints = integrals * int_mask
    panel = lax.all_gather(masked_amps, "row", axis=0, tiled=True)
    return contract(panel, lax.all_gather(masked_ints, "col", axis=1, tiled=True))


def solution(mesh):
    return jax.shard_map(
        on_device,
        mesh=mesh,
        in_specs=(P(("col", "row"), None), P("row", "col"), P("row", "col"), P("col", None)),
        out_specs=P("col", "row"),
        check_vma=False,
    )
```

profile of v0, /device:TPU:0, one launch (start us, length us, event | category | flops | bytes accessed | tf_op | source)
XLA Modules:
  0.0 279.3 jit_solution(6280737660417096425)
XLA Ops:
  6.5 0.0 copy-start.1
  6.5 0.0 all-gather.3.cloned.1.call-start
  6.5 0.7 broadcast_in_dim.12
  7.3 0.6 broadcast_in_dim.13
  7.9 2.8 %bitcast_multiply_fusion.1 = bf16[64,8192]{1,0:T(8,128)(2,1)} fusion(bf16[64,8192]{1,0:T(8,128)(2,1)} %param.4, bf16[8,8,64,128]{3,2,1,0:T(8,128)(2,1)S(1)} %bitcast.11), kind=kLoop, calls=%fused_computation.1 | loop fusion | flops 524288 | bytes 3145728 | tf_op jit(solution)/shard_map/mul | solution.py:22
  10.7 0.0 all-gather.3.cloned.1.call-update
  10.7 0.0 all-gather.5.cloned.1.call-start
  10.8 0.0 copy-done.1
  10.8 0.1 copy.5
  10.9 0.0 copy-start
  10.9 0.1 broadcast_in_dim.14
  11.0 5.8 %broadcast_in_dim.15 = bf16[2048,8,128]{2,1,0:T(8,128)(2,1)S(1)} broadcast(bf16[2048,8]{1,0:T(8,128)(2,1)S(1)} %bitcast.12), dimensions={0,1} | broadcast | bytes 4227072 | tf_op jit(solution)/shard_map/broadcast_in_dim | solution.py:23
  16.8 0.0 copy-done
  16.8 2.5 bitcast_multiply_fusion
  19.3 0.0 all-gather.5.cloned.1.call-update
  19.3 75.1 %all-gather.3.cloned.1.call-done = bf16[256,8192]{1,0:T(8,128)(2,1)} async-done(((bf16[64,8192]{1,0:T(8,128)(2,1)}), bf16[256,8192]{1,0:T(8,128)(2,1)}) %all-gather.3.cloned.1.call-update) | async-done | bytes 4194320 | tf_op jit(solution)/shard_map/all_gather | solution.py:27
  94.3 161.3 %all-gather.5.cloned.1.call-done = bf16[2048,8192]{1,0:T(8,128)(2,1)} async-done(((bf16[2048,1024]{1,0:T(8,128)(2,1)}), bf16[2048,8192]{1,0:T(8,128)(2,1)}) %all-gather.5.cloned.1.call-update) | async-done | bytes 33554448 | tf_op jit(solution)/shard_map/all_gather | solution.py:28
  255.6 16.9 %fusion = f32[256,2048]{1,0:T(8,128)} fusion(bf16[256,8192]{1,0:T(8,128)(2,1)} %all-gather.3.cloned.1.call-done, bf16[2048,8192]{1,0:T(8,128)(2,1)} %all-gather.5.cloned.1.call-done), kind=kOutput, calls=%fused_computation.3 | convolution fusion | flops 8589934592 | bytes 39845888 | tf_op jit(solution)/shard_map/dot_general | solution.py:10
  (2 shorter events, 0.0 us)
Async XLA Ops:
  6.5 4.2 %copy-start.1 = (s32[16,8]{0,1:T(8,128)S(1)}, s32[16,8]{0,1:T(8,128)}, u32[]{:S(2)}) copy-start(s32[16,8]{0,1:T(8,128)} %param.6) | copy-start | bytes 1540
  6.5 87.8 %all-gather.3.cloned.1.call-start = ((), (), s32[]{:S(2)}) async-start(), calls=%async_computation | async-start | bytes 5242880 | tf_op jit(solution)/shard_map/all_gather | solution.py:27
  10.7 244.9 %all-gather.5.cloned.1.call-start = ((), (), s32[]{:S(2)}) async-start(), calls=%async_computation.1 | async-start | bytes 37748736 | tf_op jit(solution)/shard_map/all_gather | solution.py:28
  10.9 5.9 %copy-start = (bf16[2048,1024]{1,0:T(8,128)(2,1)S(1)}, bf16[2048,1024]{1,0:T(8,128)(2,1)}, u32[]{:S(2)}) copy-start(bf16[2048,1024]{1,0:T(8,128)(2,1)} %param.5) | copy-start | bytes 12582916
Sparse Core Ops, SparseCore 0:
  10.8 83.4 all-gather.2
  96.2 159.3 all-gather.4
where the time goes:
time: 280 us; the launch traced here: 279 us
  waiting for transfers between devices  236 us (84%)
  matrix products  16.9 us (6%)
  between operations  13.5 us (5%)
  local copies, waits for them, and re-layouts  7.25 us (3%)
  other arithmetic  5.35 us (2%)
    all_gather x1, waiting for transfers between devices, on_device(): lax.all_gather(masked_ints, 'col', axis=1, tiled=True)  161 us
    all_gather x1, waiting for transfers between devices, on_device(): panel = lax.all_gather(masked_amps, 'row', axis=0, tiled=True)  75.1 us
    dot_general x1, matrix products, contract(): lax.dot_general(left, right, (((1,), (1,)), ((), ())), preferred_element_...  16.9 us
    broadcast_in_dim x1, local copies, waits for them, and re-layouts, on_device(): jnp.repeat(jnp.repeat(integral_tiles, TILE, axis=0), TILE, axis=1)  5.78 us
  transfers between devices with their start and end apart: 2, of which 2 were waited for; matrix products, arithmetic and copies ran while one was open for 3% of the time, Pallas kernels for 0%

commit v1 on v0

v1 whole, which is shorter than its diff:
```python
import functools

import jax
import jax.numpy as jnp
import numpy as np
from jax import lax
from jax.experimental import pallas as pl
from jax.experimental.pallas import tpu as pltpu
from jax.sharding import PartitionSpec as P

TILE = 128
LANES = 128
CHUNKS = 2
MIB = 1 << 20


def arrivals(rows):
    order = []
    for z in range(rows):
        mine = []
        for d in range(1, rows):
            if z + d < rows:
                mine.append((d, 1))
            if z - d >= 0:
                mine.append((d, -1))
        order.append(mine)
    return order


def split_amps(info, tiles, amps, *outs, chips, chunks, width):
    chip, tile_row = info[0], info[2]
    rows = amps.shape[0] // chunks
    per = width // TILE
    for d in range(chips):
        there = chip ^ d
        for t in range(per):
            column = pl.multiple_of(there * width + t * TILE, TILE)
            kept = tiles[tile_row, there * per + t] != 0
            block = amps[:, pl.ds(column, TILE)]
            block = jnp.where(kept, block, jnp.zeros_like(block))
            for h in range(chunks):
                outs[h * chips + d][:, t * TILE : (t + 1) * TILE] = block[h * rows : (h + 1) * rows]


def mask_ints(tiles, ints, out):
    step = pl.program_id(0)
    per = ints.shape[0] // TILE
    for r in range(per):
        for t in range(ints.shape[1] // TILE):
            kept = tiles[step * per + r, t] != 0
            block = ints[r * TILE : (r + 1) * TILE, t * TILE : (t + 1) * TILE]
            out[r * TILE : (r + 1) * TILE, t * TILE : (t + 1) * TILE] = jnp.where(kept, block, jnp.zeros_like(block))


def partial_sums(info, *refs, n_pieces, n_choices, which, chips, tn):
    pieces = refs[: n_pieces * n_choices]
    ours, theirs = refs[n_pieces * n_choices : n_pieces * n_choices + 2]
    outs = refs[n_pieces * n_choices + 2 : n_pieces * n_choices + 2 + n_pieces * chips]
    left, total = refs[-2:]
    step = pl.program_id(0)
    rows = pieces[0].shape[0]

    @pl.when(step == 0)
    def _():
        for p in range(n_pieces):
            for c in range(n_choices):
                if n_choices == 1:
                    left[p * rows : (p + 1) * rows] = pieces[p * n_choices + c][...]
                else:

                    @pl.when(info[which] == c)
                    def _():
                        left[p * rows : (p + 1) * rows] = pieces[p * n_choices + c][...]

    half = ours.shape[1]
    core = info[1]
    mine = pl.multiple_of(core * half, half)
    other = pl.multiple_of((1 - core) * half, half)
    dims = (((1,), (1,)), ((), ()))
    sums = lax.dot_general(left[:, pl.ds(mine, half)], ours[...], dims, preferred_element_type=jnp.float32)
    sums += lax.dot_general(left[:, pl.ds(other, half)], theirs[...], dims, preferred_element_type=jnp.float32)
    total[:, pl.ds(pl.multiple_of(step * tn, tn), tn)] = sums

    @pl.when(step == pl.num_programs(0) - 1)
    def _():
        one = rows // chips
        width = total.shape[1]
        for p in range(n_pieces):
            for d in range(chips):
                block = total[p * rows + d * one : p * rows + (d + 1) * one]
                out = outs[p * chips + d]
                if d == 0:
                    out[...] = block
                else:
                    top = jnp.max(jnp.abs(block), axis=1, keepdims=True)
                    power = jnp.ceil(jnp.log2(jnp.maximum(top, 2.0**-100)) + 0.01)
                    out[:, :width] = jnp.round(block * jnp.exp2(14.0 - power) * 1.98).astype(jnp.int32).astype(jnp.int16)
                    out[:, width:] = jnp.broadcast_to(power, (one, LANES)).astype(jnp.int32).astype(jnp.int16)


def add_up(info, *refs, chips):
    own, coded, out = refs[0], refs[1:chips], refs[-1]
    width = own.shape[1]
    total = own[...]
    for ref in coded:
        power = ref[:, width : width + 1].astype(jnp.int32).astype(jnp.float32)
        total += ref[:, :width].astype(jnp.int32).astype(jnp.float32) * (jnp.exp2(power - 14.0) * (1.0 / 1.98))
    out[...] = total


def call(body, name, grid, in_specs, out_specs, out_shape, scalars, args, scratch=(), flops=0, moved=0, aliases=None):
    return pl.pallas_call(
        body,
        out_shape=out_shape,
        grid_spec=pltpu.PrefetchScalarGridSpec(
            num_scalar_prefetch=len(scalars), grid=grid, in_specs=in_specs, out_specs=out_specs, scratch_shapes=list(scratch)
        ),
        compiler_params=pltpu.CompilerParams(vmem_limit_bytes=40 * MIB),
        cost_estimate=pl.CostEstimate(flops=flops, bytes_accessed=moved, transcendentals=0),
        input_output_aliases=aliases or {},
        name=name,
    )(*scalars, *args)


def whole(shape):
    return pl.BlockSpec(shape, lambda *_: (0,) * len(shape))


def on_device(n_row, n_col, amplitudes, integrals, integral_tiles, amplitude_tiles):
    chips, chunks = n_col // 2, CHUNKS
    m, cds = amplitudes.shape
    width = cds // chips
    rows = m // chunks
    nab, half = integrals.shape

    order = arrivals(n_row)
    choices, table = [], []
    for j in range(n_row - 1):
        choices.append(sorted({order[z][j] for z in range(n_row)}))
    for z in range(n_row):
        sources = [z] + [z + d * side for d, side in order[z]]
        picks = [0] + [choices[j].index(order[z][j]) for j in range(n_row - 1)]
        for c in range(n_col):
            table.append([c // 2, c % 2, z * m // TILE, *picks, *sources])
    table = np.array(table, np.int32)
    here = lax.axis_index("row") * n_col + lax.axis_index("col")
    info = lax.dynamic_index_in_dim(jnp.asarray(table), here, 0, keepdims=False)
    pick_at, source_at = 3, 3 + n_row

    def over(d):
        return [(i, i ^ (2 * d)) for i in range(n_col)]

    parts = call(
        functools.partial(split_amps, chips=chips, chunks=chunks, width=width),
        "split_amps",
        (1,),
        [whole(amplitudes.shape)],
        [whole((rows, width))] * (chips * chunks),
        [jax.ShapeDtypeStruct((rows, width), jnp.bfloat16)] * (chips * chunks),
        (info, amplitude_tiles),
        (amplitudes,),
        moved=4 * m * cds,
    )
    pieces = []
    for h in range(chunks):
        got = [parts[h * chips]]
        for d in range(1, chips):
            got.append(lax.ppermute(parts[h * chips + d], "col", over(d)))
        pieces.append(jnp.concatenate(got, axis=0))

    tall = min(512, nab)
    ours = call(
        mask_ints,
        "mask_ints",
        (nab // tall,),
        [pl.BlockSpec((tall, half), lambda i, *_: (i, 0))],
        pl.BlockSpec((tall, half), lambda i, *_: (i, 0)),
        jax.ShapeDtypeStruct(integrals.shape, jnp.bfloat16),
        (integral_tiles,),
        (integrals,),
        moved=4 * nab * half,
    )
    theirs = lax.ppermute(ours, "col", [(i, i ^ 1) for i in range(n_col)])

    came = []
    for h in range(chunks):
        held = {(0, 1): pieces[h], (0, -1): pieces[h]}
        for d in range(1, n_row):
            down = [(i + 1, i) for i in range(n_row - 1) if i + d < n_row]
            up = [(i, i + 1) for i in range(n_row - 1) if i - d + 1 >= 0]
            held[(d, 1)] = lax.ppermute(held[(d - 1, 1)], "row", down)
            held[(d, -1)] = lax.ppermute(held[(d - 1, -1)], "row", up)
        came.append(held)

    tn = min(512, nab)
    result = None
    for j in range(n_row):
        wanted = [(0, 1)] if j == 0 else choices[j - 1]
        last = j == n_row - 1
        groups = [[h] for h in range(chunks)] if last else [list(range(chunks))]
        for group in groups:
            operands = [came[h][w] for h in group for w in wanted]
            tall = chips * rows
            outs = call(
                functools.partial(
                    partial_sums, n_pieces=len(group), n_choices=len(wanted), which=pick_at + j, chips=chips, tn=tn
                ),
                "partial_sums",
                (nab // tn,),
                [whole((tall, width))] * len(operands) + [pl.BlockSpec((tn, half), lambda i, *_: (i, 0))] * 2,
                ([whole((rows, nab))] + [whole((rows, nab + LANES))] * (chips - 1)) * len(group),
                (
                    [jax.ShapeDtypeStruct((rows, nab), jnp.float32)]
                    + [jax.ShapeDtypeStruct((rows, nab + LANES), jnp.int16)] * (chips - 1)
                )
                * len(group),
                (info,),
                (*operands, ours, theirs),
                scratch=[
                    pltpu.VMEM((len(group) * tall, width), jnp.bfloat16),
                    pltpu.VMEM((len(group) * tall, nab), jnp.float32),
                ],
                flops=2 * len(group) * tall * width * nab,
                moved=4 * nab * half,
            )
            for p, h in enumerate(group):
                own = outs[p * chips]
                coded = [lax.ppermute(outs[p * chips + d], "col", over(d)) for d in range(1, chips)]
                place = lambda i, info, j=j, h=h: (info[source_at + j] * chunks + h, 0)
                body = functools.partial(add_up, chips=chips)
                specs = [whole(x.shape) for x in (own, *coded)]
                args = (own, *coded)
                aliases = {}
                if result is not None:
                    body = functools.partial(lambda f, info, base, *refs: f(info, *refs), body)
                    specs = [pl.BlockSpec(memory_space=pl.ANY)] + specs
                    args = (result, *args)
                    aliases = {1: 0}
                result = call(
                    body,
                    "add_up",
                    (1,),
                    specs,
                    pl.BlockSpec((rows, nab), place),
                    jax.ShapeDtypeStruct((n_row * m, nab), jnp.float32),
                    (info,),
                    args,
                    aliases=aliases,
                    moved=16 * rows * nab,
                )
    return result


def solution(mesh):
    return jax.shard_map(
        functools.partial(on_device, mesh.shape["row"], mesh.shape["col"]),
        mesh=mesh,
        in_specs=(P(("col", "row"), None), P("row", "col"), P("row", "col"), P("col", None)),
        out_specs=P("col", "row"),
        check_vma=False,
    )
```

time: 280 us -> 153 us (0.55)
  waiting for transfers between devices: 236 us -> 40.5 us
  starting transfers between devices: 0.04 us -> 57.4 us
  Pallas kernels: 0 us -> 48.1 us
  matrix products: 16.9 us -> 0 us
  between operations: 13.5 us -> 0.32 us
  other arithmetic: 5.35 us -> 0 us
  local copies, waits for them, and re-layouts: 7.25 us -> 3.73 us
    all_gather x2 -> x0, waiting for transfers between devices: 236 us -> none  [the longest x1 161 us: on_device(): lax.all_gather(masked_ints, 'col', axis=1, tiled=True)]
    ppermute x0 -> x43, starting transfers between devices: none -> 57.4 us  [the longest x24 28.5 us: on_device(): lax.ppermute(outs[p * chips + d], 'col', over(d))]
    pallas_call x0 -> x15, Pallas kernels: none -> 48.1 us  [call(): pl.pallas_call(body, out_shape=out_shape, grid_spec=pltpu.PrefetchScalarG...]
    ppermute x0 -> x43, waiting for transfers between devices: none -> 40.5 us  [the longest x6 30.8 us: on_device(): held[d, 1] = lax.ppermute(held[d - 1, 1], 'row', down)]
    dot_general x1 -> x0, matrix products: 16.9 us -> none  [contract(): lax.dot_general(left, right, (((1,), (1,)), ((), ())), preferred_element_...]
    broadcast_in_dim x4 -> x0, local copies, waits for them, and re-layouts: 7.16 us -> none  [the longest x1 5.78 us: on_device(): jnp.repeat(jnp.repeat(integral_tiles, TILE, axis=0), TILE, axis=1)]
    mul x2 -> x0, other arithmetic: 5.33 us -> none  [the longest x1 2.83 us: on_device(): masked_amps = amplitudes * amp_mask]
    unnamed x4 -> x13, local copies, waits for them, and re-layouts: 0.01 us -> 3.01 us
  transfers between devices with their start and end apart: 2 -> 43, of which waited for: 2 -> 9; matrix products, arithmetic and copies ran while one was open for 3% -> 1% of each run, Pallas kernels for 0% -> 29%
where the time goes in v1:
time: 153 us; the launch traced here: 150 us
  starting transfers between devices  57.4 us (38%)
  Pallas kernels  48.1 us (31%)
  waiting for transfers between devices  40.5 us (26%)
  local copies, waits for them, and re-layouts  3.73 us (2%)
    pallas_call x15, Pallas kernels, call(): pl.pallas_call(body, out_shape=out_shape, grid_spec=pltpu.PrefetchScalarG...  48.1 us
    ppermute x6, waiting for transfers between devices, on_device(): held[d, 1] = lax.ppermute(held[d - 1, 1], 'row', down)  30.8 us
    ppermute x24, starting transfers between devices, on_device(): lax.ppermute(outs[p * chips + d], 'col', over(d))  28.5 us
    ppermute x6, starting transfers between devices, on_device(): held[d, -1] = lax.ppermute(held[d - 1, -1], 'row', up)  10.8 us
    ppermute x6, starting transfers between devices, on_device(): got.append(lax.ppermute(parts[h * chips + d], 'col', over(d)))  9.99 us
    ppermute x6, starting transfers between devices, on_device(): held[d, 1] = lax.ppermute(held[d - 1, 1], 'row', down)  7.71 us
    ppermute x6, waiting for transfers between devices, on_device(): held[d, -1] = lax.ppermute(held[d - 1, -1], 'row', up)  7.11 us
  transfers between devices with their start and end apart: 43, of which 9 were waited for; matrix products, arithmetic and copies ran while one was open for 1% of the time, Pallas kernels for 29%

profile of v1, /device:TPU:0, one launch (start us, length us, event | category | flops | bytes accessed | tf_op | source)
XLA Modules:
  0.0 150.2 jit_solution(8318893692033671006)
XLA Ops:
  0.8 2.2 %copy-done = bf16[2048,1024]{1,0:T(8,128)(2,1)S(1)} copy-done((bf16[2048,1024]{1,0:T(8,128)(2,1)S(1)}, bf16[2048,1024]{1,0:T(8,128)(2,1)}, u32[]{:S(2)}) %copy-start) | copy-done | bytes 4194328
  3.0 3.6 %mask_ints.1.refs_2_.refs_4_.refs_6_ = bf16[2048,1024]{1,0:T(8,128)(2,1)} custom-call(s32[16,8]{1,0:T(8,128)S(1)} %copy.13.tiles, bf16[2048,1024]{1,0:T(8,128)(2,1)S(1)} %copy-done), custom_call_target="tpu_custom_call" | custom-call | bytes 8388608 | tf_op jit(solution)/shard_map/mask_ints/pallas_call | solution.py:112
  8.6 2.6 %collective-permute-start = (bf16[32,2048]{1,0:T(8,128)(2,1)S(1)}, bf16[32,2048]{1,0:T(8,128)(2,1)S(1)}, u32[]{:S(2)}, u32[]{:S(2)}) collective-permute-start(bf16[32,2048]{1,0:T(8,128)(2,1)S(1)} %get-tuple-element.46), channel_id=1, source_target_pairs={{0,2},{1,3},{2,0},{3,1},{4,6},{5,7},{6,4},{7,5},{8,10},{9,11},{10,... | collective-permute-start | bytes 393224 | tf_op jit(solution)/shard_map/ppermute | solution.py:168
  12.7 1.9 %collective-permute-start.3 = (bf16[32,2048]{1,0:T(8,128)(2,1)S(1)}, bf16[32,2048]{1,0:T(8,128)(2,1)S(1)}, u32[]{:S(2)}, u32[]{:S(2)}) collective-permute-start(bf16[32,2048]{1,0:T(8,128)(2,1)S(1)} %get-tuple-element.50), channel_id=1, source_target_pairs={{0,2},{1,3},{2,0},{3,1},{4,6},{5,7},{6,4},{7,5},{8,10},{9,11},{10,... | collective-permute-start | bytes 393224 | tf_op jit(solution)/shard_map/ppermute | solution.py:168
  15.4 2.1 %collective-permute-start.4 = (bf16[32,2048]{1,0:T(8,128)(2,1)S(1)}, bf16[32,2048]{1,0:T(8,128)(2,1)S(1)}, u32[]{:S(2)}, u32[]{:S(2)}) collective-permute-start(bf16[32,2048]{1,0:T(8,128)(2,1)S(1)} %get-tuple-element.51), channel_id=1, source_target_pairs={{0,4},{1,5},{2,6},{3,7},{4,0},{5,1},{6,2},{7,3},{8,12},{9,13},{10,... | collective-permute-start | bytes 393224 | tf_op jit(solution)/shard_map/ppermute | solution.py:168
  17.5 1.8 %collective-permute-done.1 = bf16[32,2048]{1,0:T(8,128)(2,1)S(1)} collective-permute-done((bf16[32,2048]{1,0:T(8,128)(2,1)S(1)}, bf16[32,2048]{1,0:T(8,128)(2,1)S(1)}, u32[]{:S(2)}, u32[]{:S(2)}) %collective-permute-start.1) | collective-permute-done | bytes 131104 | tf_op jit(solution)/shard_map/ppermute | solution.py:168
  19.4 1.9 %collective-permute-start.5 = (bf16[32,2048]{1,0:T(8,128)(2,1)S(1)}, bf16[32,2048]{1,0:T(8,128)(2,1)S(1)}, u32[]{:S(2)}, u32[]{:S(2)}) collective-permute-start(bf16[32,2048]{1,0:T(8,128)(2,1)S(1)} %get-tuple-element.52), channel_id=1, source_target_pairs={{0,6},{1,7},{2,4},{3,5},{4,2},{5,3},{6,0},{7,1},{8,14},{9,15},{10,... | collective-permute-start | bytes 393224 | tf_op jit(solution)/shard_map/ppermute | solution.py:168
  21.3 3.5 %collective-permute-start.13 = (bf16[128,2048]{1,0:T(8,128)(2,1)S(1)}, bf16[128,2048]{1,0:T(8,128)(2,1)S(1)}, u32[]{:S(2)}, u32[]{:S(2)}) collective-permute-start(bf16[128,2048]{1,0:T(8,128)(2,1)S(1)} %constant_dynamic-update-slice_fusion.refs_0_), channel_id=1, source_target_pairs={{0,8},{8,16},{16,24},{1,9},{9,17},{17,25},{2,10},{10,18},{18,26},{... | collective-permute-start | bytes 1572872 | tf_op jit(solution)/shard_map/ppermute | solution.py:192
  26.2 4.6 %collective-permute-start.15 = (bf16[128,2048]{1,0:T(8,128)(2,1)S(1)}, bf16[128,2048]{1,0:T(8,128)(2,1)S(1)}, u32[]{:S(2)}, u32[]{:S(2)}) collective-permute-start(bf16[128,2048]{1,0:T(8,128)(2,1)S(1)} %constant_dynamic-update-slice_fusion.4.refs_1_), channel_id=1, source_target_pairs={{0,8},{8,16},{16,24},{1,9},{9,17},{17,25},{2,10},{10,18},{18,26},{... | collective-permute-start | bytes 1572872 | tf_op jit(solution)/shard_map/ppermute | solution.py:192
  32.1 5.1 %collective-permute-done.13.refs_0_ = bf16[128,2048]{1,0:T(8,128)(2,1)S(1)} collective-permute-done((bf16[128,2048]{1,0:T(8,128)(2,1)S(1)}, bf16[128,2048]{1,0:T(8,128)(2,1)S(1)}, u32[]{:S(2)}, u32[]{:S(2)}) %collective-permute-start.13) | collective-permute-done | bytes 524320 | tf_op jit(solution)/shard_map/ppermute | solution.py:192
  37.8 3.7 %collective-permute-done.14.refs_1_ = bf16[128,2048]{1,0:T(8,128)(2,1)S(1)} collective-permute-done((bf16[128,2048]{1,0:T(8,128)(2,1)S(1)}, bf16[128,2048]{1,0:T(8,128)(2,1)S(1)}, u32[]{:S(2)}, u32[]{:S(2)}) %collective-permute-start.14) | collective-permute-done | bytes 524320 | tf_op jit(solution)/shard_map/ppermute | solution.py:191
  42.9 2.0 %collective-permute-done.15.refs_2_.refs_3_ = bf16[128,2048]{1,0:T(8,128)(2,1)S(1)} collective-permute-done((bf16[128,2048]{1,0:T(8,128)(2,1)S(1)}, bf16[128,2048]{1,0:T(8,128)(2,1)S(1)}, u32[]{:S(2)}, u32[]{:S(2)}) %collective-permute-start.15) | collective-permute-done | bytes 524320 | tf_op jit(solution)/shard_map/ppermute | solution.py:192
  45.6 7.2 %collective-permute-done.16.refs_3_ = bf16[128,2048]{1,0:T(8,128)(2,1)S(1)} collective-permute-done((bf16[128,2048]{1,0:T(8,128)(2,1)S(1)}, bf16[128,2048]{1,0:T(8,128)(2,1)S(1)}, u32[]{:S(2)}, u32[]{:S(2)}) %collective-permute-start.16) | collective-permute-done | bytes 524320 | tf_op jit(solution)/shard_map/ppermute | solution.py:191
  54.8 9.2 %collective-permute-done.24.refs_2_.refs_1_ = bf16[128,2048]{1,0:T(8,128)(2,1)S(1)} collective-permute-done((bf16[128,2048]{1,0:T(8,128)(2,1)S(1)}, bf16[128,2048]{1,0:T(8,128)(2,1)S(1)}, u32[]{:S(2)}, u32[]{:S(2)}) %collective-permute-start.24) | collective-permute-done | bytes 524320 | tf_op jit(solution)/shard_map/ppermute | solution.py:191
  66.0 9.2 %collective-permute-done.26.refs_5_.refs_1_ = bf16[128,2048]{1,0:T(8,128)(2,1)S(1)} collective-permute-done((bf16[128,2048]{1,0:T(8,128)(2,1)S(1)}, bf16[128,2048]{1,0:T(8,128)(2,1)S(1)}, u32[]{:S(2)}, u32[]{:S(2)}) %collective-permute-start.26) | collective-permute-done | bytes 524320 | tf_op jit(solution)/shard_map/ppermute | solution.py:191
  76.6 6.5 %partial_sums.5 = (f32[32,2048]{1,0:T(8,128)S(1)}, s16[32,2176]{1,0:T(8,128)(2,1)S(1)}, s16[32,2176]{1,0:T(8,128)(2,1)S(1)}, s16[32,2176]{1,0:T(8,128)(2,1)S(1)}...) custom-call(s32[11]{0:T(128)S(1)} %dynamic-slice_bitcast_fusion.info, ...), custom_call_target="tpu_custom_call" | custom-call | flops 2147483648 | bytes 8388608 | tf_op jit(solution)/shard_map/partial_sums/pallas_call | solution.py:112
  83.1 2.1 %collective-permute-start.7 = (s16[32,2176]{1,0:T(8,128)(2,1)S(1)}, s16[32,2176]{1,0:T(8,128)(2,1)S(1)}, u32[]{:S(2)}, u32[]{:S(2)}) collective-permute-start(s16[32,2176]{1,0:T(8,128)(2,1)S(1)} %get-tuple-element.54), channel_id=1, source_target_pairs={{0,2},{1,3},{2,0},{3,1},{4,6},{5,7},{6,4},{7,5},{8,10},{9,11},{10,... | collective-permute-start | bytes 417800 | tf_op jit(solution)/shard_map/ppermute | solution.py:228
  88.7 6.5 %partial_sums.6 = (f32[32,2048]{1,0:T(8,128)S(1)}, s16[32,2176]{1,0:T(8,128)(2,1)S(1)}, s16[32,2176]{1,0:T(8,128)(2,1)S(1)}, s16[32,2176]{1,0:T(8,128)(2,1)S(1)}...) custom-call(s32[11]{0:T(128)S(1)} %dynamic-slice_bitcast_fusion.info, ...), custom_call_target="tpu_custom_call" | custom-call | flops 2147483648 | bytes 8388608 | tf_op jit(solution)/shard_map/partial_sums/pallas_call | solution.py:112
  96.6 1.6 %collective-permute-start.12 = (s16[32,2176]{1,0:T(8,128)(2,1)S(1)}, s16[32,2176]{1,0:T(8,128)(2,1)S(1)}, u32[]{:S(2)}, u32[]{:S(2)}) collective-permute-start(s16[32,2176]{1,0:T(8,128)(2,1)S(1)} %get-tuple-element.60), channel_id=1, source_target_pairs={{0,6},{1,7},{2,4},{3,5},{4,2},{5,3},{6,0},{7,1},{8,14},{9,15},{10,... | collective-permute-start | bytes 417800 | tf_op jit(solution)/shard_map/ppermute | solution.py:228
  100.2 1.6 %collective-permute-start.19 = (s16[32,2176]{1,0:T(8,128)(2,1)S(1)}, s16[32,2176]{1,0:T(8,128)(2,1)S(1)}, u32[]{:S(2)}, u32[]{:S(2)}) collective-permute-start(s16[32,2176]{1,0:T(8,128)(2,1)S(1)} %get-tuple-element.64), channel_id=1, source_target_pairs={{0,6},{1,7},{2,4},{3,5},{4,2},{5,3},{6,0},{7,1},{8,14},{9,15},{10,... | collective-permute-start | bytes 417800 | tf_op jit(solution)/shard_map/ppermute | solution.py:228
  101.7 6.5 %partial_sums.7 = (f32[32,2048]{1,0:T(8,128)S(1)}, s16[32,2176]{1,0:T(8,128)(2,1)S(1)}, s16[32,2176]{1,0:T(8,128)(2,1)S(1)}, s16[32,2176]{1,0:T(8,128)(2,1)S(1)}...) custom-call(s32[11]{0:T(128)S(1)} %dynamic-slice_bitcast_fusion.info, ...), custom_call_target="tpu_custom_call" | custom-call | flops 2147483648 | bytes 8388608 | tf_op jit(solution)/shard_map/partial_sums/pallas_call | solution.py:112
  113.7 6.6 %partial_sums.8 = (f32[32,2048]{1,0:T(8,128)S(1)}, s16[32,2176]{1,0:T(8,128)(2,1)S(1)}, s16[32,2176]{1,0:T(8,128)(2,1)S(1)}, s16[32,2176]{1,0:T(8,128)(2,1)S(1)}) custom-call(s32[11]{0:T(128)S(1)} %dynamic-slice_bitcast_fusion.info, bf16[128,2048]{1,0:T(8,128)(2,1)S(1)} %collective-permute-done.23.refs_1_.refs_0_, ...), custom_call_target="tpu_custom_call" | custom-call | flops 1073741824 | bytes 8388608 | tf_op jit(solution)/shard_map/partial_sums/pallas_call | solution.py:112
  120.3 1.6 %collective-permute-start.29 = (s16[32,2176]{1,0:T(8,128)(2,1)S(1)}, s16[32,2176]{1,0:T(8,128)(2,1)S(1)}, u32[]{:S(2)}, u32[]{:S(2)}) collective-permute-start(s16[32,2176]{1,0:T(8,128)(2,1)S(1)} %get-tuple-element.72), channel_id=1, source_target_pairs={{0,6},{1,7},{2,4},{3,5},{4,2},{5,3},{6,0},{7,1},{8,14},{9,15},{10,... | collective-permute-start | bytes 417800 | tf_op jit(solution)/shard_map/ppermute | solution.py:228
  126.0 6.6 %partial_sums.9 = (f32[32,2048]{1,0:T(8,128)S(1)}, s16[32,2176]{1,0:T(8,128)(2,1)S(1)}, s16[32,2176]{1,0:T(8,128)(2,1)S(1)}, s16[32,2176]{1,0:T(8,128)(2,1)S(1)}) custom-call(s32[11]{0:T(128)S(1)} %dynamic-slice_bitcast_fusion.info, bf16[128,2048]{1,0:T(8,128)(2,1)S(1)} %collective-permute-done.25.refs_4_.refs_0_, ...), custom_call_target="tpu_custom_call" | custom-call | flops 1073741824 | bytes 8388608 | tf_op jit(solution)/shard_map/partial_sums/pallas_call | solution.py:112
  (93 shorter events, 49.7 us)
Async XLA Ops:
  6.6 70.0 %collective-permute-start.6 = (bf16[2048,1024]{1,0:T(8,128)(2,1)}, bf16[2048,1024]{1,0:T(8,128)(2,1)}, u32[]{:S(2)}, u32[]{:S(2)}) collective-permute-start(bf16[2048,1024]{1,0:T(8,128)(2,1)} %mask_ints.1.refs_2_.refs_4_.refs_6_), channel_id=1, source_target_pairs={{0,1},{1,0},{2,3},{3,2},{4,5},{5,4},{6,7},{7,6},{8,9},{9,8},{10,11... | collective-permute-start | bytes 12582920 | tf_op jit(solution)/shard_map/ppermute | solution.py:183
  21.3 15.9 %collective-permute-start.13 = (bf16[128,2048]{1,0:T(8,128)(2,1)S(1)}, bf16[128,2048]{1,0:T(8,128)(2,1)S(1)}, u32[]{:S(2)}, u32[]{:S(2)}) collective-permute-start(bf16[128,2048]{1,0:T(8,128)(2,1)S(1)} %constant_dynamic-update-slice_fusion.refs_0_), channel_id=1, source_target_pairs={{0,8},{8,16},{16,24},{1,9},{9,17},{17,25},{2,10},{10,18},{18,26},{... | collective-permute-start | bytes 1572872 | tf_op jit(solution)/shard_map/ppermute | solution.py:192
  24.8 16.8 %collective-permute-start.14 = (bf16[128,2048]{1,0:T(8,128)(2,1)S(1)}, bf16[128,2048]{1,0:T(8,128)(2,1)S(1)}, u32[]{:S(2)}, u32[]{:S(2)}) collective-permute-start(bf16[128,2048]{1,0:T(8,128)(2,1)S(1)} %constant_dynamic-update-slice_fusion.refs_0_), channel_id=1, source_target_pairs={{8,0},{16,8},{24,16},{9,1},{17,9},{25,17},{10,2},{18,10},{26,18},{... | collective-permute-start | bytes 1572872 | tf_op jit(solution)/shard_map/ppermute | solution.py:191
  26.2 18.7 %collective-permute-start.15 = (bf16[128,2048]{1,0:T(8,128)(2,1)S(1)}, bf16[128,2048]{1,0:T(8,128)(2,1)S(1)}, u32[]{:S(2)}, u32[]{:S(2)}) collective-permute-start(bf16[128,2048]{1,0:T(8,128)(2,1)S(1)} %constant_dynamic-update-slice_fusion.4.refs_1_), channel_id=1, source_target_pairs={{0,8},{8,16},{16,24},{1,9},{9,17},{17,25},{2,10},{10,18},{18,26},{... | collective-permute-start | bytes 1572872 | tf_op jit(solution)/shard_map/ppermute | solution.py:192
  30.8 22.0 %collective-permute-start.16 = (bf16[128,2048]{1,0:T(8,128)(2,1)S(1)}, bf16[128,2048]{1,0:T(8,128)(2,1)S(1)}, u32[]{:S(2)}, u32[]{:S(2)}) collective-permute-start(bf16[128,2048]{1,0:T(8,128)(2,1)S(1)} %constant_dynamic-update-slice_fusion.4.refs_1_), channel_id=1, source_target_pairs={{8,0},{16,8},{24,16},{9,1},{17,9},{25,17},{10,2},{18,10},{26,18},{... | collective-permute-start | bytes 1572872 | tf_op jit(solution)/shard_map/ppermute | solution.py:191
  37.1 17.0 %collective-permute-start.23 = (bf16[128,2048]{1,0:T(8,128)(2,1)S(1)}, bf16[128,2048]{1,0:T(8,128)(2,1)S(1)}, u32[]{:S(2)}, u32[]{:S(2)}) collective-permute-start(bf16[128,2048]{1,0:T(8,128)(2,1)S(1)} %collective-permute-done.13.refs_0_), channel_id=1, source_target_pairs={{8,16},{16,24},{9,17},{17,25},{10,18},{18,26},{11,19},{19,27},{12,... | collective-permute-start | bytes 1572872 | tf_op jit(solution)/shard_map/ppermute | solution.py:192
  41.6 22.5 %collective-permute-start.24 = (bf16[128,2048]{1,0:T(8,128)(2,1)S(1)}, bf16[128,2048]{1,0:T(8,128)(2,1)S(1)}, u32[]{:S(2)}, u32[]{:S(2)}) collective-permute-start(bf16[128,2048]{1,0:T(8,128)(2,1)S(1)} %collective-permute-done.14.refs_1_), channel_id=1, source_target_pairs={{8,0},{16,8},{9,1},{17,9},{10,2},{18,10},{11,3},{19,11},{12,4},{20... | collective-permute-start | bytes 1572872 | tf_op jit(solution)/shard_map/ppermute | solution.py:191
  44.9 20.4 %collective-permute-start.25 = (bf16[128,2048]{1,0:T(8,128)(2,1)S(1)}, bf16[128,2048]{1,0:T(8,128)(2,1)S(1)}, u32[]{:S(2)}, u32[]{:S(2)}) collective-permute-start(bf16[128,2048]{1,0:T(8,128)(2,1)S(1)} %collective-permute-done.15.refs_2_.refs_3_), channel_id=1, source_target_pairs={{8,16},{16,24},{9,17},{17,25},{10,18},{18,26},{11,19},{19,27},{12,... | collective-permute-start | bytes 1572872 | tf_op jit(solution)/shard_map/ppermute | solution.py:192
  52.8 22.5 %collective-permute-start.26 = (bf16[128,2048]{1,0:T(8,128)(2,1)S(1)}, bf16[128,2048]{1,0:T(8,128)(2,1)S(1)}, u32[]{:S(2)}, u32[]{:S(2)}) collective-permute-start(bf16[128,2048]{1,0:T(8,128)(2,1)S(1)} %collective-permute-done.16.refs_3_), channel_id=1, source_target_pairs={{8,0},{16,8},{9,1},{17,9},{10,2},{18,10},{11,3},{19,11},{12,4},{20... | collective-permute-start | bytes 1572872 | tf_op jit(solution)/shard_map/ppermute | solution.py:191
  54.1 31.1 %collective-permute-start.33 = (bf16[128,2048]{1,0:T(8,128)(2,1)S(1)}, bf16[128,2048]{1,0:T(8,128)(2,1)S(1)}, u32[]{:S(2)}, u32[]{:S(2)}) collective-permute-start(bf16[128,2048]{1,0:T(8,128)(2,1)S(1)} %collective-permute-done.23.refs_1_.refs_0_), channel_id=1, source_target_pairs={{16,24},{17,25},{18,26},{19,27},{20,28},{21,29},{22,30},{23,31}} | collective-permute-start | bytes 1572872 | tf_op jit(solution)/shard_map/ppermute | solution.py:192
  64.0 22.5 %collective-permute-start.34 = (bf16[128,2048]{1,0:T(8,128)(2,1)S(1)}, bf16[128,2048]{1,0:T(8,128)(2,1)S(1)}, u32[]{:S(2)}, u32[]{:S(2)}) collective-permute-start(bf16[128,2048]{1,0:T(8,128)(2,1)S(1)} %collective-permute-done.24.refs_2_.refs_1_), channel_id=1, source_target_pairs={{8,0},{9,1},{10,2},{11,3},{12,4},{13,5},{14,6},{15,7}} | collective-permute-start | bytes 1572872 | tf_op jit(solution)/shard_map/ppermute | solution.py:191
  65.3 22.2 %collective-permute-start.38 = (bf16[128,2048]{1,0:T(8,128)(2,1)S(1)}, bf16[128,2048]{1,0:T(8,128)(2,1)S(1)}, u32[]{:S(2)}, u32[]{:S(2)}) collective-permute-start(bf16[128,2048]{1,0:T(8,128)(2,1)S(1)} %collective-permute-done.25.refs_4_.refs_0_), channel_id=1, source_target_pairs={{16,24},{17,25},{18,26},{19,27},{20,28},{21,29},{22,30},{23,31}} | collective-permute-start | bytes 1572872 | tf_op jit(solution)/shard_map/ppermute | solution.py:192
  75.3 19.9 %collective-permute-start.39 = (bf16[128,2048]{1,0:T(8,128)(2,1)S(1)}, bf16[128,2048]{1,0:T(8,128)(2,1)S(1)}, u32[]{:S(2)}, u32[]{:S(2)}) collective-permute-start(bf16[128,2048]{1,0:T(8,128)(2,1)S(1)} %collective-permute-done.26.refs_5_.refs_1_), channel_id=1, source_target_pairs={{8,0},{9,1},{10,2},{11,3},{12,4},{13,5},{14,6},{15,7}} | collective-permute-start | bytes 1572872 | tf_op jit(solution)/shard_map/ppermute | solution.py:191
  83.1 13.5 %collective-permute-start.7 = (s16[32,2176]{1,0:T(8,128)(2,1)S(1)}, s16[32,2176]{1,0:T(8,128)(2,1)S(1)}, u32[]{:S(2)}, u32[]{:S(2)}) collective-permute-start(s16[32,2176]{1,0:T(8,128)(2,1)S(1)} %get-tuple-element.54), channel_id=1, source_target_pairs={{0,2},{1,3},{2,0},{3,1},{4,6},{5,7},{6,4},{7,5},{8,10},{9,11},{10,... | collective-permute-start | bytes 417800 | tf_op jit(solution)/shard_map/ppermute | solution.py:228
  85.2 13.0 %collective-permute-start.8 = (s16[32,2176]{1,0:T(8,128)(2,1)S(1)}, s16[32,2176]{1,0:T(8,128)(2,1)S(1)}, u32[]{:S(2)}, u32[]{:S(2)}) collective-permute-start(s16[32,2176]{1,0:T(8,128)(2,1)S(1)} %get-tuple-element.55), channel_id=1, source_target_pairs={{0,4},{1,5},{2,6},{3,7},{4,0},{5,1},{6,2},{7,3},{8,12},{9,13},{10,... | collective-permute-start | bytes 417800 | tf_op jit(solution)/shard_map/ppermute | solution.py:228
  95.2 13.0 %collective-permute-start.11 = (s16[32,2176]{1,0:T(8,128)(2,1)S(1)}, s16[32,2176]{1,0:T(8,128)(2,1)S(1)}, u32[]{:S(2)}, u32[]{:S(2)}) collective-permute-start(s16[32,2176]{1,0:T(8,128)(2,1)S(1)} %get-tuple-element.59), channel_id=1, source_target_pairs={{0,4},{1,5},{2,6},{3,7},{4,0},{5,1},{6,2},{7,3},{8,12},{9,13},{10,... | collective-permute-start | bytes 417800 | tf_op jit(solution)/shard_map/ppermute | solution.py:228
  98.7 13.1 %collective-permute-start.18 = (s16[32,2176]{1,0:T(8,128)(2,1)S(1)}, s16[32,2176]{1,0:T(8,128)(2,1)S(1)}, u32[]{:S(2)}, u32[]{:S(2)}) collective-permute-start(s16[32,2176]{1,0:T(8,128)(2,1)S(1)} %get-tuple-element.63), channel_id=1, source_target_pairs={{0,4},{1,5},{2,6},{3,7},{4,0},{5,1},{6,2},{7,3},{8,12},{9,13},{10,... | collective-permute-start | bytes 417800 | tf_op jit(solution)/shard_map/ppermute | solution.py:228
  108.8 13.2 %collective-permute-start.21 = (s16[32,2176]{1,0:T(8,128)(2,1)S(1)}, s16[32,2176]{1,0:T(8,128)(2,1)S(1)}, u32[]{:S(2)}, u32[]{:S(2)}) collective-permute-start(s16[32,2176]{1,0:T(8,128)(2,1)S(1)} %get-tuple-element.67), channel_id=1, source_target_pairs={{0,4},{1,5},{2,6},{3,7},{4,0},{5,1},{6,2},{7,3},{8,12},{9,13},{10,... | collective-permute-start | bytes 417800 | tf_op jit(solution)/shard_map/ppermute | solution.py:228
  112.3 13.2 %collective-permute-start.28 = (s16[32,2176]{1,0:T(8,128)(2,1)S(1)}, s16[32,2176]{1,0:T(8,128)(2,1)S(1)}, u32[]{:S(2)}, u32[]{:S(2)}) collective-permute-start(s16[32,2176]{1,0:T(8,128)(2,1)S(1)} %get-tuple-element.71), channel_id=1, source_target_pairs={{0,4},{1,5},{2,6},{3,7},{4,0},{5,1},{6,2},{7,3},{8,12},{9,13},{10,... | collective-permute-start | bytes 417800 | tf_op jit(solution)/shard_map/ppermute | solution.py:228
  122.5 13.2 %collective-permute-start.31 = (s16[32,2176]{1,0:T(8,128)(2,1)S(1)}, s16[32,2176]{1,0:T(8,128)(2,1)S(1)}, u32[]{:S(2)}, u32[]{:S(2)}) collective-permute-start(s16[32,2176]{1,0:T(8,128)(2,1)S(1)} %get-tuple-element.75), channel_id=1, source_target_pairs={{0,4},{1,5},{2,6},{3,7},{4,0},{5,1},{6,2},{7,3},{8,12},{9,13},{10,... | collective-permute-start | bytes 417800 | tf_op jit(solution)/shard_map/ppermute | solution.py:228
  132.6 14.8 %collective-permute-start.36 = (s16[32,2176]{1,0:T(8,128)(2,1)S(1)}, s16[32,2176]{1,0:T(8,128)(2,1)S(1)}, u32[]{:S(2)}, u32[]{:S(2)}) collective-permute-start(s16[32,2176]{1,0:T(8,128)(2,1)S(1)} %get-tuple-element.79), channel_id=1, source_target_pairs={{0,4},{1,5},{2,6},{3,7},{4,0},{5,1},{6,2},{7,3},{8,12},{9,13},{10,... | collective-permute-start | bytes 417800 | tf_op jit(solution)/shard_map/ppermute | solution.py:228
  134.1 13.3 %collective-permute-start.37 = (s16[32,2176]{1,0:T(8,128)(2,1)S(1)}, s16[32,2176]{1,0:T(8,128)(2,1)S(1)}, u32[]{:S(2)}, u32[]{:S(2)}) collective-permute-start(s16[32,2176]{1,0:T(8,128)(2,1)S(1)} %get-tuple-element.80), channel_id=1, source_target_pairs={{0,6},{1,7},{2,4},{3,5},{4,2},{5,3},{6,0},{7,1},{8,14},{9,15},{10,... | collective-permute-start | bytes 417800 | tf_op jit(solution)/shard_map/ppermute | solution.py:228
  135.6 13.2 %collective-permute-start.40 = (s16[32,2176]{1,0:T(8,128)(2,1)S(1)}, s16[32,2176]{1,0:T(8,128)(2,1)S(1)}, u32[]{:S(2)}, u32[]{:S(2)}) collective-permute-start(s16[32,2176]{1,0:T(8,128)(2,1)S(1)} %get-tuple-element.82), channel_id=1, source_target_pairs={{0,2},{1,3},{2,0},{3,1},{4,6},{5,7},{6,4},{7,5},{8,10},{9,11},{10,... | collective-permute-start | bytes 417800 | tf_op jit(solution)/shard_map/ppermute | solution.py:228
  136.1 12.7 %collective-permute-start.41 = (s16[32,2176]{1,0:T(8,128)(2,1)S(1)}, s16[32,2176]{1,0:T(8,128)(2,1)S(1)}, u32[]{:S(2)}, u32[]{:S(2)}) collective-permute-start(s16[32,2176]{1,0:T(8,128)(2,1)S(1)} %get-tuple-element.83), channel_id=1, source_target_pairs={{0,4},{1,5},{2,6},{3,7},{4,0},{5,1},{6,2},{7,3},{8,12},{9,13},{10,... | collective-permute-start | bytes 417800 | tf_op jit(solution)/shard_map/ppermute | solution.py:228
  (22 other events, 222.4 us)

commit v2 on v0

v2 whole, which is shorter than its diff:
```python
import functools

import jax
import jax.numpy as jnp
import numpy as np
from jax import lax
from jax.experimental import pallas as pl
from jax.experimental.pallas import tpu as pltpu
from jax.sharding import PartitionSpec as P

TILE = 128
LANES = 128
CHUNKS = 2
MIB = 1 << 20


def row_plan(rows, chunks):
    moves, slots, steps = {}, [], []
    everything = tuple(range(chunks))
    if rows == 4 and chunks == 2:
        middle, outward = [(1, 2), (2, 1)], [(1, 0), (2, 3)]
        moves = {
            "pair": ("own", [(0, 1), (1, 0), (2, 3), (3, 2)]),
            "cross": ("own", middle),
            "far": ("cross", outward),
            "cross2": ("pair", middle),
            "far2": ("cross2", outward),
        }
        slots = [
            (["pair"], [0, 0, 0, 0], [1, 0, 3, 2]),
            (["far", "cross"], [0, 1, 1, 0], [2, 2, 1, 1]),
            (["far2", "cross2"], [0, 1, 1, 0], [3, 3, 0, 0]),
        ]
        steps = [
            ("move", "cross", 0, ()),
            ("move", "pair", 0, ()),
            ("multiply", 0, everything, ()),
            ("move", "cross", 1, ()),
            ("move", "pair", 1, (("own", 0), )),
            ("move", "far", 0, ()),
            ("multiply", 1, everything, (("far", 0), )),
            ("move", "cross2", 0, (("cross", 1), )),
            ("move", "far", 1, (("own", 1), )),
            ("add", 0, (everything,)),
            ("move", "cross2", 1, ()),
            ("move", "far2", 0, (("own", 0), )),
            ("multiply", 2, everything, ()),
            ("add", 1, (everything,)),
            ("move", "far2", 1, (("own", 2), ("result",), )),
            ("multiply", 3, everything, ()),
            ("add", 2, (everything,)),
            ("add", 3, (everything,)),
        ]
        return moves, slots, steps
    order = [[] for _ in range(rows)]
    for d in range(1, rows):
        low, high = f"low{d}", f"high{d}"
        moves[high] = (f"high{d - 1}" if d > 1 else "own", [(i + 1, i) for i in range(rows - d)])
        moves[low] = (f"low{d - 1}" if d > 1 else "own", [(i, i + 1) for i in range(d - 1, rows - 1)])
        for z in range(rows):
            order[z] += [(high, z + d)] * (z + d < rows) + [(low, z - d)] * (z >= d)
        steps += [("move", name, h, ()) for name in (high, low) for h in everything]
    for j in range(rows - 1):
        names = sorted({order[z][j][0] for z in range(rows)})
        slots.append((names, [names.index(order[z][j][0]) for z in range(rows)], [order[z][j][1] for z in range(rows)]))
    steps += [("multiply", j, everything, ()) for j in range(rows)] + [("add", j, (everything,)) for j in range(rows)]
    return moves, slots, steps


def split_amps(tiles, amps, *outs, chips, starts, width):
    chip, tile_row = lax.axis_index("col") // 2, lax.axis_index("row") * amps.shape[0] // TILE
    per = width // TILE
    for d in range(chips):
        there = chip ^ d
        for t in range(per):
            column = pl.multiple_of(there * width + t * TILE, TILE)
            kept = tiles[tile_row, there * per + t] != 0
            block = amps[:, pl.ds(column, TILE)]
            block = jnp.where(kept, block, jnp.zeros_like(block))
            for h in range(len(starts) - 1):
                outs[h * chips + d][:, t * TILE : (t + 1) * TILE] = block[starts[h] : starts[h + 1]]


def masked(block, tiles, first):
    rows = []
    for r in range(block.shape[0] // TILE):
        row = []
        for t in range(block.shape[1] // TILE):
            tile = block[r * TILE : (r + 1) * TILE, t * TILE : (t + 1) * TILE]
            row.append(jnp.where(tiles[first + r, t] != 0, tile, jnp.zeros_like(tile)))
        rows.append(jnp.concatenate(row, axis=1))
    return jnp.concatenate(rows, axis=0)


def first_sums(info, our_tiles, their_tiles, piece, *refs, **kw):
    n = kw["n_pieces"] - 1
    more, (ours, theirs), outs = refs[:n], refs[n : n + 2], refs[n + 2 :]
    our_kept, their_kept = outs[-4:-2]
    first = pl.program_id(0) * (ours.shape[0] // TILE)
    our_kept[...] = masked(ours[...], our_tiles, first)
    their_kept[...] = masked(theirs[...], their_tiles, first)
    partial_sums(info, piece, *more, our_kept, their_kept, *outs[:-4], *outs[-2:], **kw)


def partial_sums(info, *refs, n_pieces, n_choices, which, chips, tn):
    pieces = refs[: n_pieces * n_choices]
    ours, theirs = refs[n_pieces * n_choices : n_pieces * n_choices + 2]
    outs = refs[n_pieces * n_choices + 2 : -2]
    left, total = refs[-2:]
    step = pl.program_id(0)
    rows = [pieces[p * n_choices].shape[0] for p in range(n_pieces)]
    at = [sum(rows[:p]) for p in range(n_pieces)]

    @pl.when(step == 0)
    def _():
        for p in range(n_pieces):
            for c in range(n_choices):

                @pl.when((info[which] == c) if n_choices > 1 else True)
                def _():
                    left[at[p] : at[p] + rows[p]] = pieces[p * n_choices + c][...]

    half = ours.shape[1]
    core = info[1]
    mine = pl.multiple_of(core * half, half)
    other = pl.multiple_of((1 - core) * half, half)
    dims = (((1,), (1,)), ((), ()))
    sums = lax.dot_general(left[:, pl.ds(mine, half)], ours[...], dims, preferred_element_type=jnp.float32)
    sums += lax.dot_general(left[:, pl.ds(other, half)], theirs[...], dims, preferred_element_type=jnp.float32)
    total[:, pl.ds(pl.multiple_of(step * tn, tn), tn)] = sums

    @pl.when(step == pl.num_programs(0) - 1)
    def _():
        for p in range(n_pieces):
            one = rows[p] // chips
            there = slice(at[p] // chips, at[p] // chips + one)
            for d in range(chips):
                block = total[at[p] + d * one : at[p] + (d + 1) * one]
                if d == 0:
                    outs[0][there] = block
                else:
                    encode(block, outs[d].at[there])


def encode(block, out):
    width = block.shape[1]
    top = jnp.max(jnp.abs(block), axis=1, keepdims=True)
    power = jnp.ceil(jnp.log2(jnp.maximum(top, 2.0**-100)) + 0.01)
    out[:, :width] = jnp.round(block * (jnp.exp2(14.0 - power) * 1.98)).astype(jnp.int32).astype(jnp.int16)
    out[:, width:] = jnp.broadcast_to(power, (block.shape[0], LANES)).astype(jnp.int32).astype(jnp.int16)


def decode(coded, width):
    power = coded[:, width : width + 1].astype(jnp.int32).astype(jnp.float32)
    return coded[:, :width].astype(jnp.int32).astype(jnp.float32) * (jnp.exp2(power - 14.0) * (1.0 / 1.98))


def add_up(info, *refs, chips):
    sets, out, at = refs[:-1], refs[-1], 0
    for g in range(0, len(sets), chips):
        total = sets[g][...]
        for d in range(1, chips):
            total += decode(sets[g + d][...], total.shape[1])
        out[at : at + total.shape[0]] = total
        at += total.shape[0]


def call(body, name, grid, in_specs, out_specs, out_shape, scalars, args, scratch=(), flops=0, moved=0, aliases=None):
    return pl.pallas_call(
        body,
        out_shape=out_shape,
        grid_spec=pltpu.PrefetchScalarGridSpec(
            num_scalar_prefetch=len(scalars), grid=grid, in_specs=in_specs, out_specs=out_specs, scratch_shapes=list(scratch)
        ),
        compiler_params=pltpu.CompilerParams(vmem_limit_bytes=24 * MIB),
        cost_estimate=pl.CostEstimate(flops=flops, bytes_accessed=0, transcendentals=0),
        input_output_aliases=aliases or {},
        name=name,
    )(*scalars, *args)


def whole(shape):
    return pl.BlockSpec(shape, lambda *_: (0,) * len(shape))


def on_device(n_row, n_col, amplitudes, integrals, integral_tiles, amplitude_tiles):
    chips, chunks = n_col // 2, CHUNKS
    m, cds = amplitudes.shape
    width = cds // chips
    starts = [0, 3 * m // 4, m]
    rows_of = [b - a for a, b in zip(starts, starts[1:])]
    nab, half = integrals.shape

    moves, slots, steps = row_plan(n_row, chunks)
    table = []
    for z in range(n_row):
        picks = [0] + [slot[1][z] for slot in slots]
        sources = [z] + [slot[2][z] for slot in slots]
        for c in range(n_col):
            table.append([c // 2, c % 2, z * m // TILE, *picks, *sources])
    table = np.array(table, np.int32)
    here = lax.axis_index("row") * n_col + lax.axis_index("col")
    info = lax.dynamic_index_in_dim(jnp.asarray(table), here, 0, keepdims=False)
    pick_at, source_at = 3, 3 + n_row

    def over(d):
        return [(i, i ^ (2 * d)) for i in range(n_col)]

    swap = [(i, i ^ 1) for i in range(n_col)]
    theirs = lax.ppermute(integrals, "col", swap)
    their_tiles = lax.ppermute(integral_tiles, "col", swap)
    kept = []

    parts = call(
        functools.partial(split_amps, chips=chips, starts=starts, width=width),
        "split_amps",
        (1,),
        [whole(amplitudes.shape)],
        [whole((rows, width)) for rows in rows_of for _ in range(chips)],
        [jax.ShapeDtypeStruct((rows, width), jnp.bfloat16) for rows in rows_of for _ in range(chips)],
        (amplitude_tiles,),
        (amplitudes,),
        moved=4 * m * cds,
    )
    pieces = []
    for h in range(chunks):
        got = [parts[h * chips]]
        for d in range(1, chips):
            part = parts[h * chips + d]
            got.append(lax.ppermute(after(part, their_tiles) if h else part, "col", over(d)))
        pieces.append(jnp.concatenate(got, axis=0))

    tn = min(512, nab)

    def multiply(j, operands, group):
        wanted = ["own"] if j == 0 else slots[j - 1][0]
        many = sum(rows_of[h] for h in group)
        block = pl.BlockSpec((tn, half), lambda i, *_: (i, 0))
        out = [((many, nab), jnp.float32)] + [((many, nab + LANES), jnp.int16)] * (chips - 1)
        outs = call(
            functools.partial(
                partial_sums if j else first_sums,
                n_pieces=len(group),
                n_choices=len(wanted),
                which=pick_at + j,
                chips=chips,
                tn=tn,
            ),
            "partial_sums" if j else "first_sums",
            (nab // tn,),
            [whole(x.shape) for x in operands] + [block] * 2,
            [whole(shape) for shape, _ in out] + ([] if j else [block] * 2),
            [jax.ShapeDtypeStruct(*x) for x in out] + ([] if j else [jax.ShapeDtypeStruct((nab, half), jnp.bfloat16)] * 2),
            (info,) if j else (info, integral_tiles, their_tiles),
            (*operands, *(kept if j else (pltpu.with_memory_space_constraint(integrals, pltpu.HBM), theirs))),
            scratch=[
                pltpu.VMEM((chips * many, width), jnp.bfloat16),
                pltpu.VMEM((chips * many, nab), jnp.float32),
            ],

        )
        if not j:
            kept.extend(outs[-2:])
        return [outs[0]] + [lax.ppermute(outs[d], "col", over(d)) for d in range(1, chips)]

    def gather(result, j, sums):
        def place(i, info):
            return (info[source_at + j], 0)

        body = functools.partial(add_up, chips=chips)
        specs = [whole(x.shape) for x in sums]
        args, aliases = tuple(sums), {}
        if result is not None:
            body = functools.partial(lambda f, info, base, *refs: f(info, *refs), body)
            specs = [pl.BlockSpec(memory_space=pl.ANY)] + specs
            args, aliases = (result, *args), {1: 0}
        return call(
            body,
            "add_up",
            (1,),
            specs,
            pl.BlockSpec((m, nab), place),
            jax.ShapeDtypeStruct((n_row * m, nab), jnp.float32),
            (info,),
            args,
            aliases=aliases,
            moved=16 * m * nab,
        )

    held = [{"own": pieces[h]} for h in range(chunks)]
    sums, result = {}, None

    def tied(value, ties):
        nonlocal result
        for kind, *at in ties:
            if kind == "result":
                value, result = lax.optimization_barrier((value, result))
            elif kind == "own":
                value = after(value, sums[at[0], tuple(range(chunks))][0])
            elif kind == "others":
                value = after(value, *sums[at[0], tuple(range(chunks))][1:])
            else:
                value = after(value, held[at[0]][kind])
        return value

    for kind, *step in steps:
        if kind == "move":
            name, h, ties = step
            sent, pairs = moves[name]
            held[h][name] = lax.ppermute(tied(held[h][sent], ties), "row", pairs)
        elif kind == "multiply":
            j, group, ties = step
            operands = [held[h][w] for h in group for w in (slots[j - 1][0] if j else ["own"])]
            operands[0] = tied(operands[0], ties)
            sums[j, group] = multiply(j, operands, group)
        else:
            j, groups = step
            result = gather(result, j, [x for group in groups for x in sums[j, group]])
    return result


def after(value, *others):
    return lax.optimization_barrier((value, *others))[0]


def solution(mesh):
    return jax.shard_map(
        functools.partial(on_device, mesh.shape["row"], mesh.shape["col"]),
        mesh=mesh,
        in_specs=(P(("col", "row"), None), P("row", "col"), P("row", "col"), P("col", None)),
        out_specs=P("col", "row"),
        check_vma=False,
    )
```

time: 280 us -> 113 us (0.40)
  waiting for transfers between devices: 236 us -> 34.8 us
  starting transfers between devices: 0.04 us -> 46.1 us
  Pallas kernels: 0 us -> 27.7 us
  matrix products: 16.9 us -> 0 us
  between operations: 13.5 us -> 0.27 us
  other arithmetic: 5.35 us -> 0 us
  local copies, waits for them, and re-layouts: 7.25 us -> 4.14 us
    all_gather x2 -> x0, waiting for transfers between devices: 236 us -> none  [the longest x1 161 us: on_device(): lax.all_gather(masked_ints, 'col', axis=1, tiled=True)]
    ppermute x0 -> x30, starting transfers between devices: none -> 46.1 us  [the longest x10 21.3 us: on_device(): held[h][name] = lax.ppermute(tied(held[h][sent], ties), 'row', pairs)]
    ppermute x0 -> x30, waiting for transfers between devices: none -> 34.8 us  [the longest x10 23.7 us: on_device(): held[h][name] = lax.ppermute(tied(held[h][sent], ties), 'row', pairs)]
    pallas_call x0 -> x9, Pallas kernels: none -> 27.7 us  [call(): pl.pallas_call(body, out_shape=out_shape, grid_spec=pltpu.PrefetchScalarG...]
    dot_general x1 -> x0, matrix products: 16.9 us -> none  [contract(): lax.dot_general(left, right, (((1,), (1,)), ((), ())), preferred_element_...]
    broadcast_in_dim x4 -> x0, local copies, waits for them, and re-layouts: 7.16 us -> none  [the longest x1 5.78 us: on_device(): jnp.repeat(jnp.repeat(integral_tiles, TILE, axis=0), TILE, axis=1)]
    mul x2 -> x0, other arithmetic: 5.33 us -> none  [the longest x1 2.83 us: on_device(): masked_amps = amplitudes * amp_mask]
    unnamed x4 -> x15, local copies, waits for them, and re-layouts: 0.01 us -> 3.42 us
  transfers between devices with their start and end apart: 2 -> 30, of which waited for: 2 -> 9; matrix products, arithmetic and copies ran while one was open for 3% -> 1% of each run, Pallas kernels for 0% -> 23%
where the time goes in v2:
time: 113 us
  starting transfers between devices  46.1 us (41%)
  waiting for transfers between devices  34.8 us (31%)
  Pallas kernels  27.7 us (25%)
  local copies, waits for them, and re-layouts  4.14 us (4%)
    pallas_call x9, Pallas kernels, call(): pl.pallas_call(body, out_shape=out_shape, grid_spec=pltpu.PrefetchScalarG...  27.7 us
    ppermute x10, waiting for transfers between devices, on_device(): held[h][name] = lax.ppermute(tied(held[h][sent], ties), 'row', pairs)  23.7 us
    ppermute x10, starting transfers between devices, on_device(): held[h][name] = lax.ppermute(tied(held[h][sent], ties), 'row', pairs)  21.3 us
    ppermute x12, starting transfers between devices, multiply(): lax.ppermute(outs[d], 'col', over(d))  14.3 us
    ppermute x6, starting transfers between devices, on_device(): lax.ppermute(after(part, their_tiles) if h else part, 'col', over(d))  9.98 us
    ppermute x12, waiting for transfers between devices, multiply(): lax.ppermute(outs[d], 'col', over(d))  6.34 us
    ppermute x6, waiting for transfers between devices, on_device(): lax.ppermute(after(part, their_tiles) if h else part, 'col', over(d))  4.79 us
    unnamed x15, local copies, waits for them, and re-layouts  3.42 us
  transfers between devices with their start and end apart: 30, of which 9 were waited for; matrix products, arithmetic and copies ran while one was open for 1% of the time, Pallas kernels for 23%

profile of v2, /device:TPU:0, one launch (start us, length us, event | category | flops | bytes accessed | tf_op | source)
XLA Modules:
  0.0 113.0 jit_solution(8196375258525372838)
XLA Ops:
  4.1 3.0 %collective-permute-start.4 = (bf16[48,2048]{1,0:T(8,128)(2,1)S(1)}, bf16[48,2048]{1,0:T(8,128)(2,1)S(1)}, u32[]{:S(2)}, u32[]{:S(2)}) collective-permute-start(bf16[48,2048]{1,0:T(8,128)(2,1)S(1)} %get-tuple-element.50), channel_id=1, source_target_pairs={{0,2},{1,3},{2,0},{3,1},{4,6},{5,7},{6,4},{7,5},{8,10},{9,11},{10,... | collective-permute-start | bytes 589832 | tf_op jit(solution)/shard_map/ppermute | solution.py:230
  8.7 2.0 %collective-permute-start.1 = (bf16[16,2048]{1,0:T(8,128)(2,1)S(1)}, bf16[16,2048]{1,0:T(8,128)(2,1)S(1)}, u32[]{:S(2)}, u32[]{:S(2)}) collective-permute-start(bf16[16,2048]{1,0:T(8,128)(2,1)S(1)} %get-tuple-element.44), channel_id=1, source_target_pairs={{0,2},{1,3},{2,0},{3,1},{4,6},{5,7},{6,4},{7,5},{8,10},{9,11},{10,... | collective-permute-start | bytes 196616 | tf_op jit(solution)/shard_map/ppermute | solution.py:230
  10.7 2.1 %collective-permute-done.4 = bf16[48,2048]{1,0:T(8,128)(2,1)S(1)} collective-permute-done((bf16[48,2048]{1,0:T(8,128)(2,1)S(1)}, bf16[48,2048]{1,0:T(8,128)(2,1)S(1)}, u32[]{:S(2)}, u32[]{:S(2)}) %collective-permute-start.4) | collective-permute-done | bytes 196640 | tf_op jit(solution)/shard_map/ppermute | solution.py:230
  12.8 2.1 %collective-permute-start.2 = (bf16[16,2048]{1,0:T(8,128)(2,1)S(1)}, bf16[16,2048]{1,0:T(8,128)(2,1)S(1)}, u32[]{:S(2)}, u32[]{:S(2)}) collective-permute-start(bf16[16,2048]{1,0:T(8,128)(2,1)S(1)} %get-tuple-element.46), channel_id=1, source_target_pairs={{0,4},{1,5},{2,6},{3,7},{4,0},{5,1},{6,2},{7,3},{8,12},{9,13},{10,... | collective-permute-start | bytes 196616 | tf_op jit(solution)/shard_map/ppermute | solution.py:230
  14.9 2.7 %collective-permute-done.5 = bf16[48,2048]{1,0:T(8,128)(2,1)S(1)} collective-permute-done((bf16[48,2048]{1,0:T(8,128)(2,1)S(1)}, bf16[48,2048]{1,0:T(8,128)(2,1)S(1)}, u32[]{:S(2)}, u32[]{:S(2)}) %collective-permute-start.5) | collective-permute-done | bytes 196640 | tf_op jit(solution)/shard_map/ppermute | solution.py:230
  19.7 4.4 %collective-permute-start.13 = (bf16[192,2048]{1,0:T(8,128)(2,1)S(1)}, bf16[192,2048]{1,0:T(8,128)(2,1)S(1)}, u32[]{:S(2)}, u32[]{:S(2)}) collective-permute-start(bf16[192,2048]{1,0:T(8,128)(2,1)S(1)} %constant_dynamic-update-slice_fusion.4.piece), channel_id=1, source_target_pairs={{0,8},{8,0},{16,24},{24,16},{1,9},{9,1},{17,25},{25,17},{2,10},{10... | collective-permute-start | bytes 2359304 | tf_op jit(solution)/shard_map/ppermute | solution.py:310
  26.9 13.1 %collective-permute-done.13.refs_0_ = bf16[192,2048]{1,0:T(8,128)(2,1)S(1)} collective-permute-done((bf16[192,2048]{1,0:T(8,128)(2,1)S(1)}, bf16[192,2048]{1,0:T(8,128)(2,1)S(1)}, u32[]{:S(2)}, u32[]{:S(2)}) %collective-permute-start.13) | collective-permute-done | bytes 786464 | tf_op jit(solution)/shard_map/ppermute | solution.py:310
  41.3 7.5 %first_sums.1 = (f32[64,2048]{1,0:T(8,128)S(1)}, s16[64,2176]{1,0:T(8,128)(2,1)S(1)}, s16[64,2176]{1,0:T(8,128)(2,1)S(1)}, s16[64,2176]{1,0:T(8,128)(2,1)S(1)}, ...) custom-call(s32[11]{0:T(128)S(1)} %dynamic-slice_bitcast_fusion.info, s32[16,8]{1,0:T(8,128)S(1)} %copy.9.our_tiles, ...), custom_call_target="tpu_custom_call" | custom-call | tf_op jit(solution)/shard_map/first_sums/pallas_call | solution.py:169
  48.9 8.9 %collective-permute-start.8 = (bf16[64,2048]{1,0:T(8,128)(2,1)S(1)}, bf16[64,2048]{1,0:T(8,128)(2,1)S(1)}, u32[]{:S(2)}, u32[]{:S(2)}) collective-permute-start(bf16[64,2048]{1,0:T(8,128)(2,1)S(1)} %constant_dynamic-update-slice_fusion.refs_0_), channel_id=1, source_target_pairs={{0,8},{8,0},{16,24},{24,16},{1,9},{9,1},{17,25},{25,17},{2,10},{10... | collective-permute-start | bytes 786440 | tf_op jit(solution)/shard_map/ppermute | solution.py:310
  62.2 3.9 %partial_sums.3 = (f32[64,2048]{1,0:T(8,128)S(1)}, s16[64,2176]{1,0:T(8,128)(2,1)S(1)}, s16[64,2176]{1,0:T(8,128)(2,1)S(1)}, s16[64,2176]{1,0:T(8,128)(2,1)S(1)}) custom-call(s32[11]{0:T(128)S(1)} %dynamic-slice_bitcast_fusion.info, bf16[192,2048]{1,0:T(8,128)(2,1)S(1)} %collective-permute-done.13.refs_0_, ...), custom_call_target="tpu_custom_call" | custom-call | tf_op jit(solution)/shard_map/partial_sums/pallas_call | solution.py:169
  68.7 1.6 %collective-permute-start.18 = (s16[64,2176]{1,0:T(8,128)(2,1)S(1)}, s16[64,2176]{1,0:T(8,128)(2,1)S(1)}, u32[]{:S(2)}, u32[]{:S(2)}) collective-permute-start(s16[64,2176]{1,0:T(8,128)(2,1)S(1)} %get-tuple-element.65), channel_id=1, source_target_pairs={{0,2},{1,3},{2,0},{3,1},{4,6},{5,7},{6,4},{7,5},{8,10},{9,11},{10,... | collective-permute-start | bytes 835592 | tf_op jit(solution)/shard_map/ppermute | solution.py:264
  70.8 1.6 %collective-permute-start.20 = (s16[64,2176]{1,0:T(8,128)(2,1)S(1)}, s16[64,2176]{1,0:T(8,128)(2,1)S(1)}, u32[]{:S(2)}, u32[]{:S(2)}) collective-permute-start(s16[64,2176]{1,0:T(8,128)(2,1)S(1)} %get-tuple-element.67), channel_id=1, source_target_pairs={{0,6},{1,7},{2,4},{3,5},{4,2},{5,3},{6,0},{7,1},{8,14},{9,15},{10,... | collective-permute-start | bytes 835592 | tf_op jit(solution)/shard_map/ppermute | solution.py:264
  72.4 4.8 %collective-permute-done.14.refs_2_ = bf16[64,2048]{1,0:T(8,128)(2,1)S(1)} collective-permute-done((bf16[64,2048]{1,0:T(8,128)(2,1)S(1)}, bf16[64,2048]{1,0:T(8,128)(2,1)S(1)}, u32[]{:S(2)}, u32[]{:S(2)}) %collective-permute-start.14) | collective-permute-done | bytes 262176 | tf_op jit(solution)/shard_map/ppermute | solution.py:310
  77.9 5.1 %partial_sums.4 = (f32[64,2048]{1,0:T(8,128)S(1)}, s16[64,2176]{1,0:T(8,128)(2,1)S(1)}, s16[64,2176]{1,0:T(8,128)(2,1)S(1)}, s16[64,2176]{1,0:T(8,128)(2,1)S(1)}) custom-call(s32[11]{0:T(128)S(1)} %dynamic-slice_bitcast_fusion.info, bf16[192,2048]{1,0:T(8,128)(2,1)} %collective-permute-done.11.refs_0_, ...), custom_call_target="tpu_custom_call" | custom-call | tf_op jit(solution)/shard_map/partial_sums/pallas_call | solution.py:169
  83.0 1.6 %collective-permute-start.21 = (s16[64,2176]{1,0:T(8,128)(2,1)S(1)}, s16[64,2176]{1,0:T(8,128)(2,1)S(1)}, u32[]{:S(2)}, u32[]{:S(2)}) collective-permute-start(s16[64,2176]{1,0:T(8,128)(2,1)S(1)} %get-tuple-element.69), channel_id=1, source_target_pairs={{0,2},{1,3},{2,0},{3,1},{4,6},{5,7},{6,4},{7,5},{8,10},{9,11},{10,... | collective-permute-start | bytes 835592 | tf_op jit(solution)/shard_map/ppermute | solution.py:264
  84.6 1.6 %add_up.4.base = f32[256,2048]{1,0:T(8,128)} custom-call(s32[11]{0:T(128)S(1)} %dynamic-slice_bitcast_fusion.info, f32[64,2048]{1,0:T(8,128)S(1)} %get-tuple-element.53.refs_0_, s16[64,2176]{1,0:T(8,128)(2,1)S(1)} %collective-permute-done.15.refs_1_, s16[64,2176]{1,0:T(8,128)(2,1)S(1)} %collective-permute-done.16.refs_2_, ...), custom_call_target="tpu_custom_call" | custom-call | tf_op jit(solution)/shard_map/add_up/pallas_call | solution.py:169
  86.2 1.6 %add_up.5.base = f32[256,2048]{1,0:T(8,128)} custom-call(s32[11]{0:T(128)S(1)} %dynamic-slice_bitcast_fusion.info, f32[256,2048]{1,0:T(8,128)} %add_up.4.base, f32[64,2048]{1,0:T(8,128)S(1)} %get-tuple-element.58.refs_0_, s16[64,2176]{1,0:T(8,128)(2,1)S(1)} %collective-permute-done.18.refs_1_, ...), custom_call_target="tpu_custom_call", output_to_operand_aliasing={{}: (1, {})} | custom-call | tf_op jit(solution)/shard_map/add_up/pallas_call | solution.py:169
  92.6 3.4 %collective-permute-done.26.refs_2_ = bf16[64,2048]{1,0:T(8,128)(2,1)S(1)} collective-permute-done((bf16[64,2048]{1,0:T(8,128)(2,1)S(1)}, bf16[64,2048]{1,0:T(8,128)(2,1)S(1)}, u32[]{:S(2)}, u32[]{:S(2)}) %collective-permute-start.26) | collective-permute-done | bytes 262176 | tf_op jit(solution)/shard_map/ppermute | solution.py:310
  96.0 3.9 %partial_sums.5 = (f32[64,2048]{1,0:T(8,128)S(1)}, s16[64,2176]{1,0:T(8,128)(2,1)S(1)}, s16[64,2176]{1,0:T(8,128)(2,1)S(1)}, s16[64,2176]{1,0:T(8,128)(2,1)S(1)}) custom-call(s32[11]{0:T(128)S(1)} %dynamic-slice_bitcast_fusion.info, bf16[192,2048]{1,0:T(8,128)(2,1)S(1)} %collective-permute-done.25.refs_0_, ...), custom_call_target="tpu_custom_call" | custom-call | tf_op jit(solution)/shard_map/partial_sums/pallas_call | solution.py:169
  101.4 2.1 %collective-permute-start.29 = (s16[64,2176]{1,0:T(8,128)(2,1)S(1)}, s16[64,2176]{1,0:T(8,128)(2,1)S(1)}, u32[]{:S(2)}, u32[]{:S(2)}) collective-permute-start(s16[64,2176]{1,0:T(8,128)(2,1)S(1)} %get-tuple-element.78), channel_id=1, source_target_pairs={{0,6},{1,7},{2,4},{3,5},{4,2},{5,3},{6,0},{7,1},{8,14},{9,15},{10,... | collective-permute-start | bytes 835592 | tf_op jit(solution)/shard_map/ppermute | solution.py:264
  103.5 1.6 %add_up.6.base = f32[256,2048]{1,0:T(8,128)} custom-call(s32[11]{0:T(128)S(1)} %dynamic-slice_bitcast_fusion.info, f32[256,2048]{1,0:T(8,128)} %add_up.5.base, f32[64,2048]{1,0:T(8,128)S(1)} %get-tuple-element.60.refs_0_, s16[64,2176]{1,0:T(8,128)(2,1)S(1)} %collective-permute-done.21.refs_1_, ...), custom_call_target="tpu_custom_call", output_to_operand_aliasing={{}: (1, {})} | custom-call | tf_op jit(solution)/shard_map/add_up/pallas_call | solution.py:169
  105.1 1.9 %collective-permute-done.27.refs_1_ = s16[64,2176]{1,0:T(8,128)(2,1)S(1)} collective-permute-done((s16[64,2176]{1,0:T(8,128)(2,1)S(1)}, s16[64,2176]{1,0:T(8,128)(2,1)S(1)}, u32[]{:S(2)}, u32[]{:S(2)}) %collective-permute-start.27) | collective-permute-done | bytes 278560 | tf_op jit(solution)/shard_map/ppermute | solution.py:264
  107.0 4.4 %collective-permute-done.28.refs_2_ = s16[64,2176]{1,0:T(8,128)(2,1)S(1)} collective-permute-done((s16[64,2176]{1,0:T(8,128)(2,1)S(1)}, s16[64,2176]{1,0:T(8,128)(2,1)S(1)}, u32[]{:S(2)}, u32[]{:S(2)}) %collective-permute-start.28) | collective-permute-done | bytes 278560 | tf_op jit(solution)/shard_map/ppermute | solution.py:264
  111.4 1.6 %add_up.7 = f32[256,2048]{1,0:T(8,128)} custom-call(s32[11]{0:T(128)S(1)} %dynamic-slice_bitcast_fusion.info, f32[256,2048]{1,0:T(8,128)} %add_up.6.base, f32[64,2048]{1,0:T(8,128)S(1)} %get-tuple-element.75.refs_0_, s16[64,2176]{1,0:T(8,128)(2,1)S(1)} %collective-permute-done.27.refs_1_, ...), custom_call_target="tpu_custom_call", output_to_operand_aliasing={{}: (1, {})} | custom-call | tf_op jit(solution)/shard_map/add_up/pallas_call | solution.py:169
  (63 shorter events, 26.2 us)
Async XLA Ops:
  0.0 41.3 %collective-permute-start.7 = (bf16[2048,1024]{1,0:T(8,128)(2,1)}, bf16[2048,1024]{1,0:T(8,128)(2,1)}, u32[]{:S(2)}, u32[]{:S(2)}) collective-permute-start(bf16[2048,1024]{1,0:T(8,128)(2,1)} %refs_1_.1), channel_id=1, source_target_pairs={{0,1},{1,0},{2,3},{3,2},{4,5},{5,4},{6,7},{7,6},{8,9},{9,8},{10,11... | collective-permute-start | bytes 12582920 | tf_op jit(solution)/shard_map/ppermute | solution.py:210
  4.1 8.7 %collective-permute-start.4 = (bf16[48,2048]{1,0:T(8,128)(2,1)S(1)}, bf16[48,2048]{1,0:T(8,128)(2,1)S(1)}, u32[]{:S(2)}, u32[]{:S(2)}) collective-permute-start(bf16[48,2048]{1,0:T(8,128)(2,1)S(1)} %get-tuple-element.50), channel_id=1, source_target_pairs={{0,2},{1,3},{2,0},{3,1},{4,6},{5,7},{6,4},{7,5},{8,10},{9,11},{10,... | collective-permute-start | bytes 589832 | tf_op jit(solution)/shard_map/ppermute | solution.py:230
  7.1 10.5 %collective-permute-start.5 = (bf16[48,2048]{1,0:T(8,128)(2,1)S(1)}, bf16[48,2048]{1,0:T(8,128)(2,1)S(1)}, u32[]{:S(2)}, u32[]{:S(2)}) collective-permute-start(bf16[48,2048]{1,0:T(8,128)(2,1)S(1)} %get-tuple-element.51), channel_id=1, source_target_pairs={{0,4},{1,5},{2,6},{3,7},{4,0},{5,1},{6,2},{7,3},{8,12},{9,13},{10,... | collective-permute-start | bytes 589832 | tf_op jit(solution)/shard_map/ppermute | solution.py:230
  8.6 10.3 %collective-permute-start.6 = (bf16[48,2048]{1,0:T(8,128)(2,1)S(1)}, bf16[48,2048]{1,0:T(8,128)(2,1)S(1)}, u32[]{:S(2)}, u32[]{:S(2)}) collective-permute-start(bf16[48,2048]{1,0:T(8,128)(2,1)S(1)} %get-tuple-element.52), channel_id=1, source_target_pairs={{0,6},{1,7},{2,4},{3,5},{4,2},{5,3},{6,0},{7,1},{8,14},{9,15},{10,... | collective-permute-start | bytes 589832 | tf_op jit(solution)/shard_map/ppermute | solution.py:230
  8.7 11.0 %collective-permute-start.1 = (bf16[16,2048]{1,0:T(8,128)(2,1)S(1)}, bf16[16,2048]{1,0:T(8,128)(2,1)S(1)}, u32[]{:S(2)}, u32[]{:S(2)}) collective-permute-start(bf16[16,2048]{1,0:T(8,128)(2,1)S(1)} %get-tuple-element.44), channel_id=1, source_target_pairs={{0,2},{1,3},{2,0},{3,1},{4,6},{5,7},{6,4},{7,5},{8,10},{9,11},{10,... | collective-permute-start | bytes 196616 | tf_op jit(solution)/shard_map/ppermute | solution.py:230
  12.8 11.3 %collective-permute-start.2 = (bf16[16,2048]{1,0:T(8,128)(2,1)S(1)}, bf16[16,2048]{1,0:T(8,128)(2,1)S(1)}, u32[]{:S(2)}, u32[]{:S(2)}) collective-permute-start(bf16[16,2048]{1,0:T(8,128)(2,1)S(1)} %get-tuple-element.46), channel_id=1, source_target_pairs={{0,4},{1,5},{2,6},{3,7},{4,0},{5,1},{6,2},{7,3},{8,12},{9,13},{10,... | collective-permute-start | bytes 196616 | tf_op jit(solution)/shard_map/ppermute | solution.py:230
  19.7 20.2 %collective-permute-start.13 = (bf16[192,2048]{1,0:T(8,128)(2,1)S(1)}, bf16[192,2048]{1,0:T(8,128)(2,1)S(1)}, u32[]{:S(2)}, u32[]{:S(2)}) collective-permute-start(bf16[192,2048]{1,0:T(8,128)(2,1)S(1)} %constant_dynamic-update-slice_fusion.4.piece), channel_id=1, source_target_pairs={{0,8},{8,0},{16,24},{24,16},{1,9},{9,1},{17,25},{25,17},{2,10},{10... | collective-permute-start | bytes 2359304 | tf_op jit(solution)/shard_map/ppermute | solution.py:310
  24.9 35.0 %collective-permute-start.11 = (bf16[192,2048]{1,0:T(8,128)(2,1)S(1)}, bf16[192,2048]{1,0:T(8,128)(2,1)}, u32[]{:S(2)}, u32[]{:S(2)}) collective-permute-start(bf16[192,2048]{1,0:T(8,128)(2,1)S(1)} %collective-permute-done.10.refs_1_), channel_id=1, source_target_pairs={{8,0},{16,24},{9,1},{17,25},{10,2},{18,26},{11,3},{19,27},{12,4},{... | collective-permute-start | bytes 2359304 | tf_op jit(solution)/shard_map/ppermute | solution.py:310
  39.9 27.5 %collective-permute-start.24 = (bf16[192,2048]{1,0:T(8,128)(2,1)S(1)}, bf16[192,2048]{1,0:T(8,128)(2,1)S(1)}, u32[]{:S(2)}, u32[]{:S(2)}) collective-permute-start(bf16[192,2048]{1,0:T(8,128)(2,1)S(1)} %collective-permute-done.13.refs_0_), channel_id=1, source_target_pairs={{8,16},{16,8},{9,17},{17,9},{10,18},{18,10},{11,19},{19,11},{12,20... | collective-permute-start | bytes 2359304 | tf_op jit(solution)/shard_map/ppermute | solution.py:310
  48.9 13.3 %collective-permute-start.8 = (bf16[64,2048]{1,0:T(8,128)(2,1)S(1)}, bf16[64,2048]{1,0:T(8,128)(2,1)S(1)}, u32[]{:S(2)}, u32[]{:S(2)}) collective-permute-start(bf16[64,2048]{1,0:T(8,128)(2,1)S(1)} %constant_dynamic-update-slice_fusion.refs_0_), channel_id=1, source_target_pairs={{0,8},{8,0},{16,24},{24,16},{1,9},{9,1},{17,25},{25,17},{2,10},{10... | collective-permute-start | bytes 786440 | tf_op jit(solution)/shard_map/ppermute | solution.py:310
  57.8 10.9 %collective-permute-start.15 = (s16[64,2176]{1,0:T(8,128)(2,1)S(1)}, s16[64,2176]{1,0:T(8,128)(2,1)S(1)}, u32[]{:S(2)}, u32[]{:S(2)}) collective-permute-start(s16[64,2176]{1,0:T(8,128)(2,1)S(1)} %get-tuple-element.62), channel_id=1, source_target_pairs={{0,2},{1,3},{2,0},{3,1},{4,6},{5,7},{6,4},{7,5},{8,10},{9,11},{10,... | collective-permute-start | bytes 835592 | tf_op jit(solution)/shard_map/ppermute | solution.py:264
  59.3 11.0 %collective-permute-start.16 = (s16[64,2176]{1,0:T(8,128)(2,1)S(1)}, s16[64,2176]{1,0:T(8,128)(2,1)S(1)}, u32[]{:S(2)}, u32[]{:S(2)}) collective-permute-start(s16[64,2176]{1,0:T(8,128)(2,1)S(1)} %get-tuple-element.63), channel_id=1, source_target_pairs={{0,4},{1,5},{2,6},{3,7},{4,0},{5,1},{6,2},{7,3},{8,12},{9,13},{10,... | collective-permute-start | bytes 835592 | tf_op jit(solution)/shard_map/ppermute | solution.py:264
  59.8 11.0 %collective-permute-start.17 = (s16[64,2176]{1,0:T(8,128)(2,1)S(1)}, s16[64,2176]{1,0:T(8,128)(2,1)S(1)}, u32[]{:S(2)}, u32[]{:S(2)}) collective-permute-start(s16[64,2176]{1,0:T(8,128)(2,1)S(1)} %get-tuple-element.64), channel_id=1, source_target_pairs={{0,6},{1,7},{2,4},{3,5},{4,2},{5,3},{6,0},{7,1},{8,14},{9,15},{10,... | collective-permute-start | bytes 835592 | tf_op jit(solution)/shard_map/ppermute | solution.py:264
  66.1 11.1 %collective-permute-start.14 = (bf16[64,2048]{1,0:T(8,128)(2,1)S(1)}, bf16[64,2048]{1,0:T(8,128)(2,1)S(1)}, u32[]{:S(2)}, u32[]{:S(2)}) collective-permute-start(bf16[64,2048]{1,0:T(8,128)(2,1)S(1)} %copy-done.2), channel_id=1, source_target_pairs={{8,0},{16,24},{9,1},{17,25},{10,2},{18,26},{11,3},{19,27},{12,4},{... | collective-permute-start | bytes 786440 | tf_op jit(solution)/shard_map/ppermute | solution.py:310
  67.4 25.1 %collective-permute-start.25 = (bf16[192,2048]{1,0:T(8,128)(2,1)S(1)}, bf16[192,2048]{1,0:T(8,128)(2,1)S(1)}, u32[]{:S(2)}, u32[]{:S(2)}) collective-permute-start(bf16[192,2048]{1,0:T(8,128)(2,1)S(1)} %collective-permute-done.24.refs_1_), channel_id=1, source_target_pairs={{8,0},{16,24},{9,1},{17,25},{10,2},{18,26},{11,3},{19,27},{12,4},{... | collective-permute-start | bytes 2359304 | tf_op jit(solution)/shard_map/ppermute | solution.py:310
  68.7 17.4 %collective-permute-start.18 = (s16[64,2176]{1,0:T(8,128)(2,1)S(1)}, s16[64,2176]{1,0:T(8,128)(2,1)S(1)}, u32[]{:S(2)}, u32[]{:S(2)}) collective-permute-start(s16[64,2176]{1,0:T(8,128)(2,1)S(1)} %get-tuple-element.65), channel_id=1, source_target_pairs={{0,2},{1,3},{2,0},{3,1},{4,6},{5,7},{6,4},{7,5},{8,10},{9,11},{10,... | collective-permute-start | bytes 835592 | tf_op jit(solution)/shard_map/ppermute | solution.py:264
  70.3 15.9 %collective-permute-start.19 = (s16[64,2176]{1,0:T(8,128)(2,1)S(1)}, s16[64,2176]{1,0:T(8,128)(2,1)S(1)}, u32[]{:S(2)}, u32[]{:S(2)}) collective-permute-start(s16[64,2176]{1,0:T(8,128)(2,1)S(1)} %get-tuple-element.66), channel_id=1, source_target_pairs={{0,4},{1,5},{2,6},{3,7},{4,0},{5,1},{6,2},{7,3},{8,12},{9,13},{10,... | collective-permute-start | bytes 835592 | tf_op jit(solution)/shard_map/ppermute | solution.py:264
  70.8 15.4 %collective-permute-start.20 = (s16[64,2176]{1,0:T(8,128)(2,1)S(1)}, s16[64,2176]{1,0:T(8,128)(2,1)S(1)}, u32[]{:S(2)}, u32[]{:S(2)}) collective-permute-start(s16[64,2176]{1,0:T(8,128)(2,1)S(1)} %get-tuple-element.67), channel_id=1, source_target_pairs={{0,6},{1,7},{2,4},{3,5},{4,2},{5,3},{6,0},{7,1},{8,14},{9,15},{10,... | collective-permute-start | bytes 835592 | tf_op jit(solution)/shard_map/ppermute | solution.py:264
  83.0 18.4 %collective-permute-start.21 = (s16[64,2176]{1,0:T(8,128)(2,1)S(1)}, s16[64,2176]{1,0:T(8,128)(2,1)S(1)}, u32[]{:S(2)}, u32[]{:S(2)}) collective-permute-start(s16[64,2176]{1,0:T(8,128)(2,1)S(1)} %get-tuple-element.69), channel_id=1, source_target_pairs={{0,2},{1,3},{2,0},{3,1},{4,6},{5,7},{6,4},{7,5},{8,10},{9,11},{10,... | collective-permute-start | bytes 835592 | tf_op jit(solution)/shard_map/ppermute | solution.py:264
  87.7 8.3 %collective-permute-start.26 = (bf16[64,2048]{1,0:T(8,128)(2,1)S(1)}, bf16[64,2048]{1,0:T(8,128)(2,1)S(1)}, u32[]{:S(2)}, u32[]{:S(2)}) collective-permute-start(bf16[64,2048]{1,0:T(8,128)(2,1)S(1)} %collective-permute-done.9.refs_3_), channel_id=1, source_target_pairs={{8,0},{16,24},{9,1},{17,25},{10,2},{18,26},{11,3},{19,27},{12,4},{... | collective-permute-start | bytes 786440 | tf_op jit(solution)/shard_map/ppermute | solution.py:310
  89.0 14.5 %collective-permute-start.22 = (s16[64,2176]{1,0:T(8,128)(2,1)S(1)}, s16[64,2176]{1,0:T(8,128)(2,1)S(1)}, u32[]{:S(2)}, u32[]{:S(2)}) collective-permute-start(s16[64,2176]{1,0:T(8,128)(2,1)S(1)} %get-tuple-element.70), channel_id=1, source_target_pairs={{0,4},{1,5},{2,6},{3,7},{4,0},{5,1},{6,2},{7,3},{8,12},{9,13},{10,... | collective-permute-start | bytes 835592 | tf_op jit(solution)/shard_map/ppermute | solution.py:264
  89.6 13.9 %collective-permute-start.23 = (s16[64,2176]{1,0:T(8,128)(2,1)S(1)}, s16[64,2176]{1,0:T(8,128)(2,1)S(1)}, u32[]{:S(2)}, u32[]{:S(2)}) collective-permute-start(s16[64,2176]{1,0:T(8,128)(2,1)S(1)} %get-tuple-element.71), channel_id=1, source_target_pairs={{0,6},{1,7},{2,4},{3,5},{4,2},{5,3},{6,0},{7,1},{8,14},{9,15},{10,... | collective-permute-start | bytes 835592 | tf_op jit(solution)/shard_map/ppermute | solution.py:264
  101.1 10.3 %collective-permute-start.28 = (s16[64,2176]{1,0:T(8,128)(2,1)S(1)}, s16[64,2176]{1,0:T(8,128)(2,1)S(1)}, u32[]{:S(2)}, u32[]{:S(2)}) collective-permute-start(s16[64,2176]{1,0:T(8,128)(2,1)S(1)} %get-tuple-element.77), channel_id=1, source_target_pairs={{0,4},{1,5},{2,6},{3,7},{4,0},{5,1},{6,2},{7,3},{8,12},{9,13},{10,... | collective-permute-start | bytes 835592 | tf_op jit(solution)/shard_map/ppermute | solution.py:264
  101.4 10.0 %collective-permute-start.29 = (s16[64,2176]{1,0:T(8,128)(2,1)S(1)}, s16[64,2176]{1,0:T(8,128)(2,1)S(1)}, u32[]{:S(2)}, u32[]{:S(2)}) collective-permute-start(s16[64,2176]{1,0:T(8,128)(2,1)S(1)} %get-tuple-element.78), channel_id=1, source_target_pairs={{0,6},{1,7},{2,4},{3,5},{4,2},{5,3},{6,0},{7,1},{8,14},{9,15},{10,... | collective-permute-start | bytes 835592 | tf_op jit(solution)/shard_map/ppermute | solution.py:264
  (10 other events, 41.2 us)

commit v3 on v2

--- a/solution.py
+++ b/solution.py
@@ -35,19 +35,19 @@
             ("move", "cross", 0, ()),
             ("move", "pair", 0, ()),
             ("multiply", 0, everything, ()),
-            ("move", "cross", 1, ()),
-            ("move", "pair", 1, (("own", 0), )),
+            ("move", "cross", 1, (("own", 0),)),
+            ("move", "pair", 1, (("own", 0),)),
             ("move", "far", 0, ()),
-            ("multiply", 1, everything, (("far", 0), )),
-            ("move", "cross2", 0, (("cross", 1), )),
-            ("move", "far", 1, (("own", 1), )),
+            ("multiply", 1, everything, (("far", 0),)),
+            ("move", "cross2", 0, (("cross", 1),)),
+            ("move", "far", 1, (("own", 1),)),
+            ("move", "cross2", 1, (("cross2", 0),)),
+            ("move", "far2", 0, (("own", 0),)),
+            ("multiply", 2, everything, ()),
+            ("move", "far2", 1, (("own", 2), ("others", 0), ("others", 1))),
+            ("multiply", 3, everything, ()),
             ("add", 0, (everything,)),
-            ("move", "cross2", 1, ()),
-            ("move", "far2", 0, (("own", 0), )),
-            ("multiply", 2, everything, ()),
             ("add", 1, (everything,)),
-            ("move", "far2", 1, (("own", 2), ("result",), )),
-            ("multiply", 3, everything, ()),
             ("add", 2, (everything,)),
             ("add", 3, (everything,)),
         ]
@@ -257,7 +257,6 @@
                 pltpu.VMEM((chips * many, width), jnp.bfloat16),
                 pltpu.VMEM((chips * many, nab), jnp.float32),
             ],
-
         )
         if not j:
             kept.extend(outs[-2:])

time: 113 us -> 108 us (0.956)
  waiting for transfers between devices: 34.8 us -> 31.6 us
    ppermute x12, waiting for transfers between devices: 6.34 us -> 1.87 us  [multiply(): lax.ppermute(outs[d], 'col', over(d))]
    ppermute x10, starting transfers between devices: 21.3 us -> 22.8 us  [on_device(): held[h][name] = lax.ppermute(tied(held[h][sent], ties), 'row', pairs)]
    ppermute x12, starting transfers between devices: 14.3 us -> 13 us  [multiply(): lax.ppermute(outs[d], 'col', over(d))]
    unnamed x15 -> x11, local copies, waits for them, and re-layouts: 3.42 us -> 2.72 us
where the time goes in v3:
time: 108 us
  starting transfers between devices  46.1 us (43%)
  waiting for transfers between devices  31.6 us (29%)
  Pallas kernels  26.6 us (25%)
  local copies, waits for them, and re-layouts  3.44 us (3%)
    pallas_call x9, Pallas kernels, call(): pl.pallas_call(body, out_shape=out_shape, grid_spec=pltpu.PrefetchScalarG...  26.6 us
    ppermute x10, waiting for transfers between devices, on_device(): held[h][name] = lax.ppermute(tied(held[h][sent], ties), 'row', pairs)  24.2 us
    ppermute x10, starting transfers between devices, on_device(): held[h][name] = lax.ppermute(tied(held[h][sent], ties), 'row', pairs)  22.8 us
    ppermute x12, starting transfers between devices, multiply(): lax.ppermute(outs[d], 'col', over(d))  13 us
    ppermute x6, starting transfers between devices, on_device(): lax.ppermute(after(part, their_tiles) if h else part, 'col', over(d))  9.91 us
    ppermute x6, waiting for transfers between devices, on_device(): lax.ppermute(after(part, their_tiles) if h else part, 'col', over(d))  5.54 us
    unnamed x11, local copies, waits for them, and re-layouts  2.72 us
  transfers between devices with their start and end apart: 30, of which 9 were waited for; matrix products, arithmetic and copies ran while one was open for 1% of the time, Pallas kernels for 23%

profile of v3, /device:TPU:0, one launch (start us, length us, event | category | flops | bytes accessed | tf_op | source)
XLA Modules:
  0.0 108.1 jit_solution(17066814606058891541)
XLA Ops:
  4.1 3.0 %collective-permute-start.1 = (bf16[48,2048]{1,0:T(8,128)(2,1)S(1)}, bf16[48,2048]{1,0:T(8,128)(2,1)S(1)}, u32[]{:S(2)}, u32[]{:S(2)}) collective-permute-start(bf16[48,2048]{1,0:T(8,128)(2,1)S(1)} %get-tuple-element.44), channel_id=1, source_target_pairs={{0,2},{1,3},{2,0},{3,1},{4,6},{5,7},{6,4},{7,5},{8,10},{9,11},{10,... | collective-permute-start | bytes 589832 | tf_op jit(solution)/shard_map/ppermute | solution.py:230
  9.4 1.9 %collective-permute-start.4 = (bf16[16,2048]{1,0:T(8,128)(2,1)S(1)}, bf16[16,2048]{1,0:T(8,128)(2,1)S(1)}, u32[]{:S(2)}, u32[]{:S(2)}) collective-permute-start(bf16[16,2048]{1,0:T(8,128)(2,1)S(1)} %get-tuple-element.49), channel_id=1, source_target_pairs={{0,2},{1,3},{2,0},{3,1},{4,6},{5,7},{6,4},{7,5},{8,10},{9,11},{10,... | collective-permute-start | bytes 196616 | tf_op jit(solution)/shard_map/ppermute | solution.py:230
  12.8 2.1 %collective-permute-start.5 = (bf16[16,2048]{1,0:T(8,128)(2,1)S(1)}, bf16[16,2048]{1,0:T(8,128)(2,1)S(1)}, u32[]{:S(2)}, u32[]{:S(2)}) collective-permute-start(bf16[16,2048]{1,0:T(8,128)(2,1)S(1)} %get-tuple-element.51), channel_id=1, source_target_pairs={{0,4},{1,5},{2,6},{3,7},{4,0},{5,1},{6,2},{7,3},{8,12},{9,13},{10,... | collective-permute-start | bytes 196616 | tf_op jit(solution)/shard_map/ppermute | solution.py:230
  14.9 2.7 %collective-permute-done.2 = bf16[48,2048]{1,0:T(8,128)(2,1)S(1)} collective-permute-done((bf16[48,2048]{1,0:T(8,128)(2,1)S(1)}, bf16[48,2048]{1,0:T(8,128)(2,1)S(1)}, u32[]{:S(2)}, u32[]{:S(2)}) %collective-permute-start.2) | collective-permute-done | bytes 196640 | tf_op jit(solution)/shard_map/ppermute | solution.py:230
  19.0 1.6 %collective-permute-start.11 = (bf16[192,2048]{1,0:T(8,128)(2,1)S(1)}, bf16[192,2048]{1,0:T(8,128)(2,1)S(1)}, u32[]{:S(2)}, u32[]{:S(2)}) collective-permute-start(bf16[192,2048]{1,0:T(8,128)(2,1)S(1)} %constant_dynamic-update-slice_fusion.piece), channel_id=1, source_target_pairs={{0,8},{8,0},{16,24},{24,16},{1,9},{9,1},{17,25},{25,17},{2,10},{10... | collective-permute-start | bytes 2359304 | tf_op jit(solution)/shard_map/ppermute | solution.py:309
  22.8 7.5 %first_sums.1 = (f32[64,2048]{1,0:T(8,128)S(1)}, s16[64,2176]{1,0:T(8,128)(2,1)S(1)}, s16[64,2176]{1,0:T(8,128)(2,1)S(1)}, s16[64,2176]{1,0:T(8,128)(2,1)S(1)}, ...) custom-call(s32[11]{0:T(128)S(1)} %dynamic-slice_bitcast_fusion.info, s32[16,8]{1,0:T(8,128)S(1)} %copy.10.our_tiles, ...), custom_call_target="tpu_custom_call" | custom-call | tf_op jit(solution)/shard_map/first_sums/pallas_call | solution.py:169
  32.3 4.0 %collective-permute-done.11.refs_0_ = bf16[192,2048]{1,0:T(8,128)(2,1)S(1)} collective-permute-done((bf16[192,2048]{1,0:T(8,128)(2,1)S(1)}, bf16[192,2048]{1,0:T(8,128)(2,1)S(1)}, u32[]{:S(2)}, u32[]{:S(2)}) %collective-permute-start.11) | collective-permute-done | bytes 786464 | tf_op jit(solution)/shard_map/ppermute | solution.py:309
  37.0 13.2 %collective-permute-start.14 = (bf16[64,2048]{1,0:T(8,128)(2,1)S(1)}, bf16[64,2048]{1,0:T(8,128)(2,1)S(1)}, u32[]{:S(2)}, u32[]{:S(2)}) collective-permute-start(bf16[64,2048]{1,0:T(8,128)(2,1)S(1)} %constant_dynamic-update-slice_fusion.4.refs_0_), channel_id=1, source_target_pairs={{0,8},{8,0},{16,24},{24,16},{1,9},{9,1},{17,25},{25,17},{2,10},{10... | collective-permute-start | bytes 786440 | tf_op jit(solution)/shard_map/ppermute | solution.py:309
  52.4 7.2 %collective-permute-done.13.refs_0_ = bf16[192,2048]{1,0:T(8,128)(2,1)S(1)} collective-permute-done((bf16[192,2048]{1,0:T(8,128)(2,1)S(1)}, bf16[192,2048]{1,0:T(8,128)(2,1)S(1)}, u32[]{:S(2)}, u32[]{:S(2)}) %collective-permute-start.13) | collective-permute-done | bytes 786464 | tf_op jit(solution)/shard_map/ppermute | solution.py:309
  59.6 2.8 %collective-permute-done.14.refs_1_ = bf16[64,2048]{1,0:T(8,128)(2,1)S(1)} collective-permute-done((bf16[64,2048]{1,0:T(8,128)(2,1)S(1)}, bf16[64,2048]{1,0:T(8,128)(2,1)S(1)}, u32[]{:S(2)}, u32[]{:S(2)}) %collective-permute-start.14) | collective-permute-done | bytes 262176 | tf_op jit(solution)/shard_map/ppermute | solution.py:309
  62.4 3.9 %partial_sums.3 = (f32[64,2048]{1,0:T(8,128)S(1)}, s16[64,2176]{1,0:T(8,128)(2,1)S(1)}, s16[64,2176]{1,0:T(8,128)(2,1)S(1)}, s16[64,2176]{1,0:T(8,128)(2,1)S(1)}) custom-call(s32[11]{0:T(128)S(1)} %dynamic-slice_bitcast_fusion.info, bf16[192,2048]{1,0:T(8,128)(2,1)S(1)} %collective-permute-done.11.refs_0_, ...), custom_call_target="tpu_custom_call" | custom-call | tf_op jit(solution)/shard_map/partial_sums/pallas_call | solution.py:169
  70.6 1.9 %collective-permute-start.17 = (s16[64,2176]{1,0:T(8,128)(2,1)S(1)}, s16[64,2176]{1,0:T(8,128)(2,1)S(1)}, u32[]{:S(2)}, u32[]{:S(2)}) collective-permute-start(s16[64,2176]{1,0:T(8,128)(2,1)S(1)} %get-tuple-element.65), channel_id=1, source_target_pairs={{0,6},{1,7},{2,4},{3,5},{4,2},{5,3},{6,0},{7,1},{8,14},{9,15},{10,... | collective-permute-start | bytes 835592 | tf_op jit(solution)/shard_map/ppermute | solution.py:263
  72.5 5.0 %collective-permute-done.19.refs_2_ = bf16[64,2048]{1,0:T(8,128)(2,1)S(1)} collective-permute-done((bf16[64,2048]{1,0:T(8,128)(2,1)S(1)}, bf16[64,2048]{1,0:T(8,128)(2,1)S(1)}, u32[]{:S(2)}, u32[]{:S(2)}) %collective-permute-start.19) | collective-permute-done | bytes 262176 | tf_op jit(solution)/shard_map/ppermute | solution.py:309
  78.1 3.9 %partial_sums.4 = (f32[64,2048]{1,0:T(8,128)S(1)}, s16[64,2176]{1,0:T(8,128)(2,1)S(1)}, s16[64,2176]{1,0:T(8,128)(2,1)S(1)}, s16[64,2176]{1,0:T(8,128)(2,1)S(1)}) custom-call(s32[11]{0:T(128)S(1)} %dynamic-slice_bitcast_fusion.info, bf16[192,2048]{1,0:T(8,128)(2,1)S(1)} %collective-permute-done.13.refs_0_, ...), custom_call_target="tpu_custom_call" | custom-call | tf_op jit(solution)/shard_map/partial_sums/pallas_call | solution.py:169
  83.5 2.0 %collective-permute-start.21 = (s16[64,2176]{1,0:T(8,128)(2,1)S(1)}, s16[64,2176]{1,0:T(8,128)(2,1)S(1)}, u32[]{:S(2)}, u32[]{:S(2)}) collective-permute-start(s16[64,2176]{1,0:T(8,128)(2,1)S(1)} %get-tuple-element.69), channel_id=1, source_target_pairs={{0,4},{1,5},{2,6},{3,7},{4,0},{5,1},{6,2},{7,3},{8,12},{9,13},{10,... | collective-permute-start | bytes 835592 | tf_op jit(solution)/shard_map/ppermute | solution.py:263
  85.5 1.7 %collective-permute-start.22 = (s16[64,2176]{1,0:T(8,128)(2,1)S(1)}, s16[64,2176]{1,0:T(8,128)(2,1)S(1)}, u32[]{:S(2)}, u32[]{:S(2)}) collective-permute-start(s16[64,2176]{1,0:T(8,128)(2,1)S(1)} %get-tuple-element.70), channel_id=1, source_target_pairs={{0,6},{1,7},{2,4},{3,5},{4,2},{5,3},{6,0},{7,1},{8,14},{9,15},{10,... | collective-permute-start | bytes 835592 | tf_op jit(solution)/shard_map/ppermute | solution.py:263
  87.2 5.2 %collective-permute-done.26.refs_2_ = bf16[64,2048]{1,0:T(8,128)(2,1)S(1)} collective-permute-done((bf16[64,2048]{1,0:T(8,128)(2,1)S(1)}, bf16[64,2048]{1,0:T(8,128)(2,1)S(1)}, u32[]{:S(2)}, u32[]{:S(2)}) %collective-permute-start.26) | collective-permute-done | bytes 262176 | tf_op jit(solution)/shard_map/ppermute | solution.py:309
  92.4 3.9 %partial_sums.5 = (f32[64,2048]{1,0:T(8,128)S(1)}, s16[64,2176]{1,0:T(8,128)(2,1)S(1)}, s16[64,2176]{1,0:T(8,128)(2,1)S(1)}, s16[64,2176]{1,0:T(8,128)(2,1)S(1)}) custom-call(s32[11]{0:T(128)S(1)} %dynamic-slice_bitcast_fusion.info, bf16[192,2048]{1,0:T(8,128)(2,1)S(1)} %collective-permute-done.24.refs_0_, ...), custom_call_target="tpu_custom_call" | custom-call | tf_op jit(solution)/shard_map/partial_sums/pallas_call | solution.py:169
  97.4 2.5 %collective-permute-start.29 = (s16[64,2176]{1,0:T(8,128)(2,1)S(1)}, s16[64,2176]{1,0:T(8,128)(2,1)S(1)}, u32[]{:S(2)}, u32[]{:S(2)}) collective-permute-start(s16[64,2176]{1,0:T(8,128)(2,1)S(1)} %get-tuple-element.80), channel_id=1, source_target_pairs={{0,6},{1,7},{2,4},{3,5},{4,2},{5,3},{6,0},{7,1},{8,14},{9,15},{10,... | collective-permute-start | bytes 835592 | tf_op jit(solution)/shard_map/ppermute | solution.py:263
  99.9 1.6 %add_up.4.base = f32[256,2048]{1,0:T(8,128)} custom-call(s32[11]{0:T(128)S(1)} %dynamic-slice_bitcast_fusion.info, f32[64,2048]{1,0:T(8,128)S(1)} %get-tuple-element.54.refs_0_, s16[64,2176]{1,0:T(8,128)(2,1)S(1)} %collective-permute-done.8.refs_1_, s16[64,2176]{1,0:T(8,128)(2,1)S(1)} %collective-permute-done.9.refs_2_, ...), custom_call_target="tpu_custom_call" | custom-call | tf_op jit(solution)/shard_map/add_up/pallas_call | solution.py:169
  101.5 1.6 %add_up.5.base = f32[256,2048]{1,0:T(8,128)} custom-call(s32[11]{0:T(128)S(1)} %dynamic-slice_bitcast_fusion.info, f32[256,2048]{1,0:T(8,128)} %add_up.4.base, f32[64,2048]{1,0:T(8,128)S(1)} %get-tuple-element.62.refs_0_, s16[64,2176]{1,0:T(8,128)(2,1)S(1)} %collective-permute-done.15.refs_1_, ...), custom_call_target="tpu_custom_call", output_to_operand_aliasing={{}: (1, {})} | custom-call | tf_op jit(solution)/shard_map/add_up/pallas_call | solution.py:169
  103.1 1.6 %add_up.6.base = f32[256,2048]{1,0:T(8,128)} custom-call(s32[11]{0:T(128)S(1)} %dynamic-slice_bitcast_fusion.info, f32[256,2048]{1,0:T(8,128)} %add_up.5.base, f32[64,2048]{1,0:T(8,128)S(1)} %get-tuple-element.67.refs_0_, s16[64,2176]{1,0:T(8,128)(2,1)S(1)} %collective-permute-done.20.refs_1_, ...), custom_call_target="tpu_custom_call", output_to_operand_aliasing={{}: (1, {})} | custom-call | tf_op jit(solution)/shard_map/add_up/pallas_call | solution.py:169
  104.6 1.8 %collective-permute-done.28.refs_2_ = s16[64,2176]{1,0:T(8,128)(2,1)S(1)} collective-permute-done((s16[64,2176]{1,0:T(8,128)(2,1)S(1)}, s16[64,2176]{1,0:T(8,128)(2,1)S(1)}, u32[]{:S(2)}, u32[]{:S(2)}) %collective-permute-start.28) | collective-permute-done | bytes 278560 | tf_op jit(solution)/shard_map/ppermute | solution.py:263
  106.5 1.6 %add_up.7 = f32[256,2048]{1,0:T(8,128)} custom-call(s32[11]{0:T(128)S(1)} %dynamic-slice_bitcast_fusion.info, f32[256,2048]{1,0:T(8,128)} %add_up.6.base, f32[64,2048]{1,0:T(8,128)S(1)} %get-tuple-element.77.refs_0_, s16[64,2176]{1,0:T(8,128)(2,1)S(1)} %collective-permute-done.27.refs_1_, ...), custom_call_target="tpu_custom_call", output_to_operand_aliasing={{}: (1, {})} | custom-call | tf_op jit(solution)/shard_map/add_up/pallas_call | solution.py:169
  (59 shorter events, 23.5 us)
Async XLA Ops:
  0.0 22.8 %collective-permute-start.7 = (bf16[2048,1024]{1,0:T(8,128)(2,1)}, bf16[2048,1024]{1,0:T(8,128)(2,1)}, u32[]{:S(2)}, u32[]{:S(2)}) collective-permute-start(bf16[2048,1024]{1,0:T(8,128)(2,1)} %refs_1_.1), channel_id=1, source_target_pairs={{0,1},{1,0},{2,3},{3,2},{4,5},{5,4},{6,7},{7,6},{8,9},{9,8},{10,11... | collective-permute-start | bytes 12582920 | tf_op jit(solution)/shard_map/ppermute | solution.py:210
  4.1 8.7 %collective-permute-start.1 = (bf16[48,2048]{1,0:T(8,128)(2,1)S(1)}, bf16[48,2048]{1,0:T(8,128)(2,1)S(1)}, u32[]{:S(2)}, u32[]{:S(2)}) collective-permute-start(bf16[48,2048]{1,0:T(8,128)(2,1)S(1)} %get-tuple-element.44), channel_id=1, source_target_pairs={{0,2},{1,3},{2,0},{3,1},{4,6},{5,7},{6,4},{7,5},{8,10},{9,11},{10,... | collective-permute-start | bytes 589832 | tf_op jit(solution)/shard_map/ppermute | solution.py:230
  7.1 10.5 %collective-permute-start.2 = (bf16[48,2048]{1,0:T(8,128)(2,1)S(1)}, bf16[48,2048]{1,0:T(8,128)(2,1)S(1)}, u32[]{:S(2)}, u32[]{:S(2)}) collective-permute-start(bf16[48,2048]{1,0:T(8,128)(2,1)S(1)} %get-tuple-element.45), channel_id=1, source_target_pairs={{0,4},{1,5},{2,6},{3,7},{4,0},{5,1},{6,2},{7,3},{8,12},{9,13},{10,... | collective-permute-start | bytes 589832 | tf_op jit(solution)/shard_map/ppermute | solution.py:230
  8.6 10.3 %collective-permute-start.3 = (bf16[48,2048]{1,0:T(8,128)(2,1)S(1)}, bf16[48,2048]{1,0:T(8,128)(2,1)S(1)}, u32[]{:S(2)}, u32[]{:S(2)}) collective-permute-start(bf16[48,2048]{1,0:T(8,128)(2,1)S(1)} %get-tuple-element.46), channel_id=1, source_target_pairs={{0,6},{1,7},{2,4},{3,5},{4,2},{5,3},{6,0},{7,1},{8,14},{9,15},{10,... | collective-permute-start | bytes 589832 | tf_op jit(solution)/shard_map/ppermute | solution.py:230
  9.4 11.2 %collective-permute-start.4 = (bf16[16,2048]{1,0:T(8,128)(2,1)S(1)}, bf16[16,2048]{1,0:T(8,128)(2,1)S(1)}, u32[]{:S(2)}, u32[]{:S(2)}) collective-permute-start(bf16[16,2048]{1,0:T(8,128)(2,1)S(1)} %get-tuple-element.49), channel_id=1, source_target_pairs={{0,2},{1,3},{2,0},{3,1},{4,6},{5,7},{6,4},{7,5},{8,10},{9,11},{10,... | collective-permute-start | bytes 196616 | tf_op jit(solution)/shard_map/ppermute | solution.py:230
  19.0 17.3 %collective-permute-start.11 = (bf16[192,2048]{1,0:T(8,128)(2,1)S(1)}, bf16[192,2048]{1,0:T(8,128)(2,1)S(1)}, u32[]{:S(2)}, u32[]{:S(2)}) collective-permute-start(bf16[192,2048]{1,0:T(8,128)(2,1)S(1)} %constant_dynamic-update-slice_fusion.piece), channel_id=1, source_target_pairs={{0,8},{8,0},{16,24},{24,16},{1,9},{9,1},{17,25},{25,17},{2,10},{10... | collective-permute-start | bytes 2359304 | tf_op jit(solution)/shard_map/ppermute | solution.py:309
  20.6 10.4 %collective-permute-start.12 = (bf16[192,2048]{1,0:T(8,128)(2,1)S(1)}, bf16[192,2048]{1,0:T(8,128)(2,1)S(1)}, u32[]{:S(2)}, u32[]{:S(2)}) collective-permute-start(bf16[192,2048]{1,0:T(8,128)(2,1)S(1)} %constant_dynamic-update-slice_fusion.piece), channel_id=1, source_target_pairs={{8,16},{16,8},{9,17},{17,9},{10,18},{18,10},{11,19},{19,11},{12,20... | collective-permute-start | bytes 2359304 | tf_op jit(solution)/shard_map/ppermute | solution.py:309
  31.0 28.6 %collective-permute-start.13 = (bf16[192,2048]{1,0:T(8,128)(2,1)S(1)}, bf16[192,2048]{1,0:T(8,128)(2,1)S(1)}, u32[]{:S(2)}, u32[]{:S(2)}) collective-permute-start(bf16[192,2048]{1,0:T(8,128)(2,1)S(1)} %collective-permute-done.12.refs_1_), channel_id=1, source_target_pairs={{8,0},{16,24},{9,1},{17,25},{10,2},{18,26},{11,3},{19,27},{12,4},{... | collective-permute-start | bytes 2359304 | tf_op jit(solution)/shard_map/ppermute | solution.py:309
  36.3 31.3 %collective-permute-start.23 = (bf16[192,2048]{1,0:T(8,128)(2,1)S(1)}, bf16[192,2048]{1,0:T(8,128)(2,1)S(1)}, u32[]{:S(2)}, u32[]{:S(2)}) collective-permute-start(bf16[192,2048]{1,0:T(8,128)(2,1)S(1)} %collective-permute-done.11.refs_0_), channel_id=1, source_target_pairs={{8,16},{16,8},{9,17},{17,9},{10,18},{18,10},{11,19},{19,11},{12,20... | collective-permute-start | bytes 2359304 | tf_op jit(solution)/shard_map/ppermute | solution.py:309
  37.0 25.4 %collective-permute-start.14 = (bf16[64,2048]{1,0:T(8,128)(2,1)S(1)}, bf16[64,2048]{1,0:T(8,128)(2,1)S(1)}, u32[]{:S(2)}, u32[]{:S(2)}) collective-permute-start(bf16[64,2048]{1,0:T(8,128)(2,1)S(1)} %constant_dynamic-update-slice_fusion.4.refs_0_), channel_id=1, source_target_pairs={{0,8},{8,0},{16,24},{24,16},{1,9},{9,1},{17,25},{25,17},{2,10},{10... | collective-permute-start | bytes 786440 | tf_op jit(solution)/shard_map/ppermute | solution.py:309
  50.2 18.7 %collective-permute-start.10 = (s16[64,2176]{1,0:T(8,128)(2,1)S(1)}, s16[64,2176]{1,0:T(8,128)(2,1)S(1)}, u32[]{:S(2)}, u32[]{:S(2)}) collective-permute-start(s16[64,2176]{1,0:T(8,128)(2,1)S(1)} %get-tuple-element.57), channel_id=1, source_target_pairs={{0,6},{1,7},{2,4},{3,5},{4,2},{5,3},{6,0},{7,1},{8,14},{9,15},{10,... | collective-permute-start | bytes 835592 | tf_op jit(solution)/shard_map/ppermute | solution.py:263
  51.8 17.3 %collective-permute-start.8 = (s16[64,2176]{1,0:T(8,128)(2,1)S(1)}, s16[64,2176]{1,0:T(8,128)(2,1)S(1)}, u32[]{:S(2)}, u32[]{:S(2)}) collective-permute-start(s16[64,2176]{1,0:T(8,128)(2,1)S(1)} %get-tuple-element.55), channel_id=1, source_target_pairs={{0,2},{1,3},{2,0},{3,1},{4,6},{5,7},{6,4},{7,5},{8,10},{9,11},{10,... | collective-permute-start | bytes 835592 | tf_op jit(solution)/shard_map/ppermute | solution.py:263
  59.6 11.0 %collective-permute-start.9 = (s16[64,2176]{1,0:T(8,128)(2,1)S(1)}, s16[64,2176]{1,0:T(8,128)(2,1)S(1)}, u32[]{:S(2)}, u32[]{:S(2)}) collective-permute-start(s16[64,2176]{1,0:T(8,128)(2,1)S(1)} %get-tuple-element.56), channel_id=1, source_target_pairs={{0,4},{1,5},{2,6},{3,7},{4,0},{5,1},{6,2},{7,3},{8,12},{9,13},{10,... | collective-permute-start | bytes 835592 | tf_op jit(solution)/shard_map/ppermute | solution.py:263
  66.3 11.1 %collective-permute-start.19 = (bf16[64,2048]{1,0:T(8,128)(2,1)S(1)}, bf16[64,2048]{1,0:T(8,128)(2,1)S(1)}, u32[]{:S(2)}, u32[]{:S(2)}) collective-permute-start(bf16[64,2048]{1,0:T(8,128)(2,1)S(1)} %collective-permute-done.18.refs_3_), channel_id=1, source_target_pairs={{8,0},{16,24},{9,1},{17,25},{10,2},{18,26},{11,3},{19,27},{12,4},{... | collective-permute-start | bytes 786440 | tf_op jit(solution)/shard_map/ppermute | solution.py:309
  67.6 24.7 %collective-permute-start.24 = (bf16[192,2048]{1,0:T(8,128)(2,1)S(1)}, bf16[192,2048]{1,0:T(8,128)(2,1)S(1)}, u32[]{:S(2)}, u32[]{:S(2)}) collective-permute-start(bf16[192,2048]{1,0:T(8,128)(2,1)S(1)} %collective-permute-done.23.refs_1_), channel_id=1, source_target_pairs={{8,0},{16,24},{9,1},{17,25},{10,2},{18,26},{11,3},{19,27},{12,4},{... | collective-permute-start | bytes 2359304 | tf_op jit(solution)/shard_map/ppermute | solution.py:309
  69.0 13.2 %collective-permute-start.15 = (s16[64,2176]{1,0:T(8,128)(2,1)S(1)}, s16[64,2176]{1,0:T(8,128)(2,1)S(1)}, u32[]{:S(2)}, u32[]{:S(2)}) collective-permute-start(s16[64,2176]{1,0:T(8,128)(2,1)S(1)} %get-tuple-element.63), channel_id=1, source_target_pairs={{0,2},{1,3},{2,0},{3,1},{4,6},{5,7},{6,4},{7,5},{8,10},{9,11},{10,... | collective-permute-start | bytes 835592 | tf_op jit(solution)/shard_map/ppermute | solution.py:263
  69.0 13.1 %collective-permute-start.16 = (s16[64,2176]{1,0:T(8,128)(2,1)S(1)}, s16[64,2176]{1,0:T(8,128)(2,1)S(1)}, u32[]{:S(2)}, u32[]{:S(2)}) collective-permute-start(s16[64,2176]{1,0:T(8,128)(2,1)S(1)} %get-tuple-element.64), channel_id=1, source_target_pairs={{0,4},{1,5},{2,6},{3,7},{4,0},{5,1},{6,2},{7,3},{8,12},{9,13},{10,... | collective-permute-start | bytes 835592 | tf_op jit(solution)/shard_map/ppermute | solution.py:263
  70.6 11.6 %collective-permute-start.17 = (s16[64,2176]{1,0:T(8,128)(2,1)S(1)}, s16[64,2176]{1,0:T(8,128)(2,1)S(1)}, u32[]{:S(2)}, u32[]{:S(2)}) collective-permute-start(s16[64,2176]{1,0:T(8,128)(2,1)S(1)} %get-tuple-element.65), channel_id=1, source_target_pairs={{0,6},{1,7},{2,4},{3,5},{4,2},{5,3},{6,0},{7,1},{8,14},{9,15},{10,... | collective-permute-start | bytes 835592 | tf_op jit(solution)/shard_map/ppermute | solution.py:263
  82.1 15.3 %collective-permute-start.20 = (s16[64,2176]{1,0:T(8,128)(2,1)S(1)}, s16[64,2176]{1,0:T(8,128)(2,1)S(1)}, u32[]{:S(2)}, u32[]{:S(2)}) collective-permute-start(s16[64,2176]{1,0:T(8,128)(2,1)S(1)} %get-tuple-element.68), channel_id=1, source_target_pairs={{0,2},{1,3},{2,0},{3,1},{4,6},{5,7},{6,4},{7,5},{8,10},{9,11},{10,... | collective-permute-start | bytes 835592 | tf_op jit(solution)/shard_map/ppermute | solution.py:263
  82.2 10.2 %collective-permute-start.26 = (bf16[64,2048]{1,0:T(8,128)(2,1)S(1)}, bf16[64,2048]{1,0:T(8,128)(2,1)S(1)}, u32[]{:S(2)}, u32[]{:S(2)}) collective-permute-start(bf16[64,2048]{1,0:T(8,128)(2,1)S(1)} %collective-permute-done.25.refs_3_), channel_id=1, source_target_pairs={{8,0},{16,24},{9,1},{17,25},{10,2},{18,26},{11,3},{19,27},{12,4},{... | collective-permute-start | bytes 786440 | tf_op jit(solution)/shard_map/ppermute | solution.py:309
  83.5 19.5 %collective-permute-start.21 = (s16[64,2176]{1,0:T(8,128)(2,1)S(1)}, s16[64,2176]{1,0:T(8,128)(2,1)S(1)}, u32[]{:S(2)}, u32[]{:S(2)}) collective-permute-start(s16[64,2176]{1,0:T(8,128)(2,1)S(1)} %get-tuple-element.69), channel_id=1, source_target_pairs={{0,4},{1,5},{2,6},{3,7},{4,0},{5,1},{6,2},{7,3},{8,12},{9,13},{10,... | collective-permute-start | bytes 835592 | tf_op jit(solution)/shard_map/ppermute | solution.py:263
  85.5 17.6 %collective-permute-start.22 = (s16[64,2176]{1,0:T(8,128)(2,1)S(1)}, s16[64,2176]{1,0:T(8,128)(2,1)S(1)}, u32[]{:S(2)}, u32[]{:S(2)}) collective-permute-start(s16[64,2176]{1,0:T(8,128)(2,1)S(1)} %get-tuple-element.70), channel_id=1, source_target_pairs={{0,6},{1,7},{2,4},{3,5},{4,2},{5,3},{6,0},{7,1},{8,14},{9,15},{10,... | collective-permute-start | bytes 835592 | tf_op jit(solution)/shard_map/ppermute | solution.py:263
  96.9 9.5 %collective-permute-start.28 = (s16[64,2176]{1,0:T(8,128)(2,1)S(1)}, s16[64,2176]{1,0:T(8,128)(2,1)S(1)}, u32[]{:S(2)}, u32[]{:S(2)}) collective-permute-start(s16[64,2176]{1,0:T(8,128)(2,1)S(1)} %get-tuple-element.79), channel_id=1, source_target_pairs={{0,4},{1,5},{2,6},{3,7},{4,0},{5,1},{6,2},{7,3},{8,12},{9,13},{10,... | collective-permute-start | bytes 835592 | tf_op jit(solution)/shard_map/ppermute | solution.py:263
  97.4 9.1 %collective-permute-start.29 = (s16[64,2176]{1,0:T(8,128)(2,1)S(1)}, s16[64,2176]{1,0:T(8,128)(2,1)S(1)}, u32[]{:S(2)}, u32[]{:S(2)}) collective-permute-start(s16[64,2176]{1,0:T(8,128)(2,1)S(1)} %get-tuple-element.80), channel_id=1, source_target_pairs={{0,6},{1,7},{2,4},{3,5},{4,2},{5,3},{6,0},{7,1},{8,14},{9,15},{10,... | collective-permute-start | bytes 835592 | tf_op jit(solution)/shard_map/ppermute | solution.py:263
  (8 other events, 42.8 us)

commit v4 on v3

--- a/solution.py
+++ b/solution.py
@@ -230,7 +230,7 @@
             got.append(lax.ppermute(after(part, their_tiles) if h else part, "col", over(d)))
         pieces.append(jnp.concatenate(got, axis=0))
 
-    tn = min(512, nab)
+    tn = min(1024, nab)
 
     def multiply(j, operands, group):
         wanted = ["own"] if j == 0 else slots[j - 1][0]

time: 108 us -> 108 us (level)
  Pallas kernels: 26.6 us -> 25 us
  waiting for transfers between devices: 31.6 us -> 32.7 us
    pallas_call x9, Pallas kernels: 26.6 us -> 25 us  [call(): pl.pallas_call(body, out_shape=out_shape, grid_spec=pltpu.PrefetchScalarG...]
    ppermute x12, waiting for transfers between devices: 1.87 us -> 3.01 us  [multiply(): lax.ppermute(outs[d], 'col', over(d))]
  transfers between devices with their start and end apart: 30 -> 30, of which waited for: 9 -> 11; matrix products, arithmetic and copies ran while one was open for 1% -> 1% of each run, Pallas kernels for 23% -> 22%
where the time goes in v4:
time: 108 us; the launch traced here: 107 us
  starting transfers between devices  46 us (43%)
  waiting for transfers between devices  32.7 us (30%)
  Pallas kernels  25 us (23%)
  local copies, waits for them, and re-layouts  3.44 us (3%)
    pallas_call x9, Pallas kernels, call(): pl.pallas_call(body, out_shape=out_shape, grid_spec=pltpu.PrefetchScalarG...  25 us
    ppermute x10, waiting for transfers between devices, on_device(): held[h][name] = lax.ppermute(tied(held[h][sent], ties), 'row', pairs)  24.1 us
    ppermute x10, starting transfers between devices, on_device(): held[h][name] = lax.ppermute(tied(held[h][sent], ties), 'row', pairs)  22.8 us
    ppermute x12, starting transfers between devices, multiply(): lax.ppermute(outs[d], 'col', over(d))  12.8 us
    ppermute x6, starting transfers between devices, on_device(): lax.ppermute(after(part, their_tiles) if h else part, 'col', over(d))  9.91 us
    ppermute x6, waiting for transfers between devices, on_device(): lax.ppermute(after(part, their_tiles) if h else part, 'col', over(d))  5.54 us
    ppermute x12, waiting for transfers between devices, multiply(): lax.ppermute(outs[d], 'col', over(d))  3.01 us
    unnamed x11, local copies, waits for them, and re-layouts  2.72 us
  transfers between devices with their start and end apart: 30, of which 11 were waited for; matrix products, arithmetic and copies ran while one was open for 1% of the time, Pallas kernels for 22%

profile of v4, /device:TPU:0, one launch (start us, length us, event | category | flops | bytes accessed | tf_op | source)
XLA Modules:
  0.0 107.4 jit_solution(15407509289959518323)
XLA Ops:
  4.1 3.0 %collective-permute-start.1 = (bf16[48,2048]{1,0:T(8,128)(2,1)S(1)}, bf16[48,2048]{1,0:T(8,128)(2,1)S(1)}, u32[]{:S(2)}, u32[]{:S(2)}) collective-permute-start(bf16[48,2048]{1,0:T(8,128)(2,1)S(1)} %get-tuple-element.44), channel_id=1, source_target_pairs={{0,2},{1,3},{2,0},{3,1},{4,6},{5,7},{6,4},{7,5},{8,10},{9,11},{10,... | collective-permute-start | bytes 589832 | tf_op jit(solution)/shard_map/ppermute | solution.py:230
  9.4 1.9 %collective-permute-start.4 = (bf16[16,2048]{1,0:T(8,128)(2,1)S(1)}, bf16[16,2048]{1,0:T(8,128)(2,1)S(1)}, u32[]{:S(2)}, u32[]{:S(2)}) collective-permute-start(bf16[16,2048]{1,0:T(8,128)(2,1)S(1)} %get-tuple-element.49), channel_id=1, source_target_pairs={{0,2},{1,3},{2,0},{3,1},{4,6},{5,7},{6,4},{7,5},{8,10},{9,11},{10,... | collective-permute-start | bytes 196616 | tf_op jit(solution)/shard_map/ppermute | solution.py:230
  12.8 2.1 %collective-permute-start.5 = (bf16[16,2048]{1,0:T(8,128)(2,1)S(1)}, bf16[16,2048]{1,0:T(8,128)(2,1)S(1)}, u32[]{:S(2)}, u32[]{:S(2)}) collective-permute-start(bf16[16,2048]{1,0:T(8,128)(2,1)S(1)} %get-tuple-element.51), channel_id=1, source_target_pairs={{0,4},{1,5},{2,6},{3,7},{4,0},{5,1},{6,2},{7,3},{8,12},{9,13},{10,... | collective-permute-start | bytes 196616 | tf_op jit(solution)/shard_map/ppermute | solution.py:230
  14.9 2.7 %collective-permute-done.2 = bf16[48,2048]{1,0:T(8,128)(2,1)S(1)} collective-permute-done((bf16[48,2048]{1,0:T(8,128)(2,1)S(1)}, bf16[48,2048]{1,0:T(8,128)(2,1)S(1)}, u32[]{:S(2)}, u32[]{:S(2)}) %collective-permute-start.2) | collective-permute-done | bytes 196640 | tf_op jit(solution)/shard_map/ppermute | solution.py:230
  19.0 1.6 %collective-permute-start.11 = (bf16[192,2048]{1,0:T(8,128)(2,1)S(1)}, bf16[192,2048]{1,0:T(8,128)(2,1)S(1)}, u32[]{:S(2)}, u32[]{:S(2)}) collective-permute-start(bf16[192,2048]{1,0:T(8,128)(2,1)S(1)} %constant_dynamic-update-slice_fusion.piece), channel_id=1, source_target_pairs={{0,8},{8,0},{16,24},{24,16},{1,9},{9,1},{17,25},{25,17},{2,10},{10... | collective-permute-start | bytes 2359304 | tf_op jit(solution)/shard_map/ppermute | solution.py:309
  22.8 7.2 %first_sums.1 = (f32[64,2048]{1,0:T(8,128)S(1)}, s16[64,2176]{1,0:T(8,128)(2,1)S(1)}, s16[64,2176]{1,0:T(8,128)(2,1)S(1)}, s16[64,2176]{1,0:T(8,128)(2,1)S(1)}, ...) custom-call(s32[11]{0:T(128)S(1)} %dynamic-slice_bitcast_fusion.info, s32[16,8]{1,0:T(8,128)S(1)} %copy.10.our_tiles, ...), custom_call_target="tpu_custom_call" | custom-call | tf_op jit(solution)/shard_map/first_sums/pallas_call | solution.py:169
  31.9 4.4 %collective-permute-done.11.refs_0_ = bf16[192,2048]{1,0:T(8,128)(2,1)S(1)} collective-permute-done((bf16[192,2048]{1,0:T(8,128)(2,1)S(1)}, bf16[192,2048]{1,0:T(8,128)(2,1)S(1)}, u32[]{:S(2)}, u32[]{:S(2)}) %collective-permute-start.11) | collective-permute-done | bytes 786464 | tf_op jit(solution)/shard_map/ppermute | solution.py:309
  37.0 13.2 %collective-permute-start.14 = (bf16[64,2048]{1,0:T(8,128)(2,1)S(1)}, bf16[64,2048]{1,0:T(8,128)(2,1)S(1)}, u32[]{:S(2)}, u32[]{:S(2)}) collective-permute-start(bf16[64,2048]{1,0:T(8,128)(2,1)S(1)} %constant_dynamic-update-slice_fusion.4.refs_0_), channel_id=1, source_target_pairs={{0,8},{8,0},{16,24},{24,16},{1,9},{9,1},{17,25},{25,17},{2,10},{10... | collective-permute-start | bytes 786440 | tf_op jit(solution)/shard_map/ppermute | solution.py:309
  52.4 7.2 %collective-permute-done.13.refs_0_ = bf16[192,2048]{1,0:T(8,128)(2,1)S(1)} collective-permute-done((bf16[192,2048]{1,0:T(8,128)(2,1)S(1)}, bf16[192,2048]{1,0:T(8,128)(2,1)S(1)}, u32[]{:S(2)}, u32[]{:S(2)}) %collective-permute-start.13) | collective-permute-done | bytes 786464 | tf_op jit(solution)/shard_map/ppermute | solution.py:309
  59.6 2.8 %collective-permute-done.14.refs_1_ = bf16[64,2048]{1,0:T(8,128)(2,1)S(1)} collective-permute-done((bf16[64,2048]{1,0:T(8,128)(2,1)S(1)}, bf16[64,2048]{1,0:T(8,128)(2,1)S(1)}, u32[]{:S(2)}, u32[]{:S(2)}) %collective-permute-start.14) | collective-permute-done | bytes 262176 | tf_op jit(solution)/shard_map/ppermute | solution.py:309
  62.4 3.5 %partial_sums.3 = (f32[64,2048]{1,0:T(8,128)S(1)}, s16[64,2176]{1,0:T(8,128)(2,1)S(1)}, s16[64,2176]{1,0:T(8,128)(2,1)S(1)}, s16[64,2176]{1,0:T(8,128)(2,1)S(1)}) custom-call(s32[11]{0:T(128)S(1)} %dynamic-slice_bitcast_fusion.info, bf16[192,2048]{1,0:T(8,128)(2,1)S(1)} %collective-permute-done.11.refs_0_, ...), custom_call_target="tpu_custom_call" | custom-call | tf_op jit(solution)/shard_map/partial_sums/pallas_call | solution.py:169
  70.5 1.6 %collective-permute-start.17 = (s16[64,2176]{1,0:T(8,128)(2,1)S(1)}, s16[64,2176]{1,0:T(8,128)(2,1)S(1)}, u32[]{:S(2)}, u32[]{:S(2)}) collective-permute-start(s16[64,2176]{1,0:T(8,128)(2,1)S(1)} %get-tuple-element.65), channel_id=1, source_target_pairs={{0,6},{1,7},{2,4},{3,5},{4,2},{5,3},{6,0},{7,1},{8,14},{9,15},{10,... | collective-permute-start | bytes 835592 | tf_op jit(solution)/shard_map/ppermute | solution.py:263
  72.1 5.0 %collective-permute-done.19.refs_2_ = bf16[64,2048]{1,0:T(8,128)(2,1)S(1)} collective-permute-done((bf16[64,2048]{1,0:T(8,128)(2,1)S(1)}, bf16[64,2048]{1,0:T(8,128)(2,1)S(1)}, u32[]{:S(2)}, u32[]{:S(2)}) %collective-permute-start.19) | collective-permute-done | bytes 262176 | tf_op jit(solution)/shard_map/ppermute | solution.py:309
  77.7 3.5 %partial_sums.4 = (f32[64,2048]{1,0:T(8,128)S(1)}, s16[64,2176]{1,0:T(8,128)(2,1)S(1)}, s16[64,2176]{1,0:T(8,128)(2,1)S(1)}, s16[64,2176]{1,0:T(8,128)(2,1)S(1)}) custom-call(s32[11]{0:T(128)S(1)} %dynamic-slice_bitcast_fusion.info, bf16[192,2048]{1,0:T(8,128)(2,1)S(1)} %collective-permute-done.13.refs_0_, ...), custom_call_target="tpu_custom_call" | custom-call | tf_op jit(solution)/shard_map/partial_sums/pallas_call | solution.py:169
  83.5 2.0 %collective-permute-start.21 = (s16[64,2176]{1,0:T(8,128)(2,1)S(1)}, s16[64,2176]{1,0:T(8,128)(2,1)S(1)}, u32[]{:S(2)}, u32[]{:S(2)}) collective-permute-start(s16[64,2176]{1,0:T(8,128)(2,1)S(1)} %get-tuple-element.69), channel_id=1, source_target_pairs={{0,4},{1,5},{2,6},{3,7},{4,0},{5,1},{6,2},{7,3},{8,12},{9,13},{10,... | collective-permute-start | bytes 835592 | tf_op jit(solution)/shard_map/ppermute | solution.py:263
  85.5 1.8 %collective-permute-start.22 = (s16[64,2176]{1,0:T(8,128)(2,1)S(1)}, s16[64,2176]{1,0:T(8,128)(2,1)S(1)}, u32[]{:S(2)}, u32[]{:S(2)}) collective-permute-start(s16[64,2176]{1,0:T(8,128)(2,1)S(1)} %get-tuple-element.70), channel_id=1, source_target_pairs={{0,6},{1,7},{2,4},{3,5},{4,2},{5,3},{6,0},{7,1},{8,14},{9,15},{10,... | collective-permute-start | bytes 835592 | tf_op jit(solution)/shard_map/ppermute | solution.py:263
  87.2 4.8 %collective-permute-done.26.refs_2_ = bf16[64,2048]{1,0:T(8,128)(2,1)S(1)} collective-permute-done((bf16[64,2048]{1,0:T(8,128)(2,1)S(1)}, bf16[64,2048]{1,0:T(8,128)(2,1)S(1)}, u32[]{:S(2)}, u32[]{:S(2)}) %collective-permute-start.26) | collective-permute-done | bytes 262176 | tf_op jit(solution)/shard_map/ppermute | solution.py:309
  92.0 3.5 %partial_sums.5 = (f32[64,2048]{1,0:T(8,128)S(1)}, s16[64,2176]{1,0:T(8,128)(2,1)S(1)}, s16[64,2176]{1,0:T(8,128)(2,1)S(1)}, s16[64,2176]{1,0:T(8,128)(2,1)S(1)}) custom-call(s32[11]{0:T(128)S(1)} %dynamic-slice_bitcast_fusion.info, bf16[192,2048]{1,0:T(8,128)(2,1)S(1)} %collective-permute-done.24.refs_0_, ...), custom_call_target="tpu_custom_call" | custom-call | tf_op jit(solution)/shard_map/partial_sums/pallas_call | solution.py:169
  96.5 2.5 %collective-permute-start.29 = (s16[64,2176]{1,0:T(8,128)(2,1)S(1)}, s16[64,2176]{1,0:T(8,128)(2,1)S(1)}, u32[]{:S(2)}, u32[]{:S(2)}) collective-permute-start(s16[64,2176]{1,0:T(8,128)(2,1)S(1)} %get-tuple-element.80), channel_id=1, source_target_pairs={{0,6},{1,7},{2,4},{3,5},{4,2},{5,3},{6,0},{7,1},{8,14},{9,15},{10,... | collective-permute-start | bytes 835592 | tf_op jit(solution)/shard_map/ppermute | solution.py:263
  99.1 1.6 %add_up.4.base = f32[256,2048]{1,0:T(8,128)} custom-call(s32[11]{0:T(128)S(1)} %dynamic-slice_bitcast_fusion.info, f32[64,2048]{1,0:T(8,128)S(1)} %get-tuple-element.54.refs_0_, s16[64,2176]{1,0:T(8,128)(2,1)S(1)} %collective-permute-done.8.refs_1_, s16[64,2176]{1,0:T(8,128)(2,1)S(1)} %collective-permute-done.9.refs_2_, ...), custom_call_target="tpu_custom_call" | custom-call | tf_op jit(solution)/shard_map/add_up/pallas_call | solution.py:169
  100.7 1.6 %add_up.5.base = f32[256,2048]{1,0:T(8,128)} custom-call(s32[11]{0:T(128)S(1)} %dynamic-slice_bitcast_fusion.info, f32[256,2048]{1,0:T(8,128)} %add_up.4.base, f32[64,2048]{1,0:T(8,128)S(1)} %get-tuple-element.62.refs_0_, s16[64,2176]{1,0:T(8,128)(2,1)S(1)} %collective-permute-done.15.refs_1_, ...), custom_call_target="tpu_custom_call", output_to_operand_aliasing={{}: (1, {})} | custom-call | tf_op jit(solution)/shard_map/add_up/pallas_call | solution.py:169
  102.2 1.6 %add_up.6.base = f32[256,2048]{1,0:T(8,128)} custom-call(s32[11]{0:T(128)S(1)} %dynamic-slice_bitcast_fusion.info, f32[256,2048]{1,0:T(8,128)} %add_up.5.base, f32[64,2048]{1,0:T(8,128)S(1)} %get-tuple-element.67.refs_0_, s16[64,2176]{1,0:T(8,128)(2,1)S(1)} %collective-permute-done.20.refs_1_, ...), custom_call_target="tpu_custom_call", output_to_operand_aliasing={{}: (1, {})} | custom-call | tf_op jit(solution)/shard_map/add_up/pallas_call | solution.py:169
  103.8 1.9 %collective-permute-done.28.refs_2_ = s16[64,2176]{1,0:T(8,128)(2,1)S(1)} collective-permute-done((s16[64,2176]{1,0:T(8,128)(2,1)S(1)}, s16[64,2176]{1,0:T(8,128)(2,1)S(1)}, u32[]{:S(2)}, u32[]{:S(2)}) %collective-permute-start.28) | collective-permute-done | bytes 278560 | tf_op jit(solution)/shard_map/ppermute | solution.py:263
  105.8 1.6 %add_up.7 = f32[256,2048]{1,0:T(8,128)} custom-call(s32[11]{0:T(128)S(1)} %dynamic-slice_bitcast_fusion.info, f32[256,2048]{1,0:T(8,128)} %add_up.6.base, f32[64,2048]{1,0:T(8,128)S(1)} %get-tuple-element.77.refs_0_, s16[64,2176]{1,0:T(8,128)(2,1)S(1)} %collective-permute-done.27.refs_1_, ...), custom_call_target="tpu_custom_call", output_to_operand_aliasing={{}: (1, {})} | custom-call | tf_op jit(solution)/shard_map/add_up/pallas_call | solution.py:169
  (59 shorter events, 24.5 us)
Async XLA Ops:
  0.0 22.8 %collective-permute-start.7 = (bf16[2048,1024]{1,0:T(8,128)(2,1)}, bf16[2048,1024]{1,0:T(8,128)(2,1)}, u32[]{:S(2)}, u32[]{:S(2)}) collective-permute-start(bf16[2048,1024]{1,0:T(8,128)(2,1)} %refs_1_.1), channel_id=1, source_target_pairs={{0,1},{1,0},{2,3},{3,2},{4,5},{5,4},{6,7},{7,6},{8,9},{9,8},{10,11... | collective-permute-start | bytes 12582920 | tf_op jit(solution)/shard_map/ppermute | solution.py:210
  4.1 8.7 %collective-permute-start.1 = (bf16[48,2048]{1,0:T(8,128)(2,1)S(1)}, bf16[48,2048]{1,0:T(8,128)(2,1)S(1)}, u32[]{:S(2)}, u32[]{:S(2)}) collective-permute-start(bf16[48,2048]{1,0:T(8,128)(2,1)S(1)} %get-tuple-element.44), channel_id=1, source_target_pairs={{0,2},{1,3},{2,0},{3,1},{4,6},{5,7},{6,4},{7,5},{8,10},{9,11},{10,... | collective-permute-start | bytes 589832 | tf_op jit(solution)/shard_map/ppermute | solution.py:230
  7.1 10.5 %collective-permute-start.2 = (bf16[48,2048]{1,0:T(8,128)(2,1)S(1)}, bf16[48,2048]{1,0:T(8,128)(2,1)S(1)}, u32[]{:S(2)}, u32[]{:S(2)}) collective-permute-start(bf16[48,2048]{1,0:T(8,128)(2,1)S(1)} %get-tuple-element.45), channel_id=1, source_target_pairs={{0,4},{1,5},{2,6},{3,7},{4,0},{5,1},{6,2},{7,3},{8,12},{9,13},{10,... | collective-permute-start | bytes 589832 | tf_op jit(solution)/shard_map/ppermute | solution.py:230
  8.6 10.3 %collective-permute-start.3 = (bf16[48,2048]{1,0:T(8,128)(2,1)S(1)}, bf16[48,2048]{1,0:T(8,128)(2,1)S(1)}, u32[]{:S(2)}, u32[]{:S(2)}) collective-permute-start(bf16[48,2048]{1,0:T(8,128)(2,1)S(1)} %get-tuple-element.46), channel_id=1, source_target_pairs={{0,6},{1,7},{2,4},{3,5},{4,2},{5,3},{6,0},{7,1},{8,14},{9,15},{10,... | collective-permute-start | bytes 589832 | tf_op jit(solution)/shard_map/ppermute | solution.py:230
  9.4 11.2 %collective-permute-start.4 = (bf16[16,2048]{1,0:T(8,128)(2,1)S(1)}, bf16[16,2048]{1,0:T(8,128)(2,1)S(1)}, u32[]{:S(2)}, u32[]{:S(2)}) collective-permute-start(bf16[16,2048]{1,0:T(8,128)(2,1)S(1)} %get-tuple-element.49), channel_id=1, source_target_pairs={{0,2},{1,3},{2,0},{3,1},{4,6},{5,7},{6,4},{7,5},{8,10},{9,11},{10,... | collective-permute-start | bytes 196616 | tf_op jit(solution)/shard_map/ppermute | solution.py:230
  19.0 17.3 %collective-permute-start.11 = (bf16[192,2048]{1,0:T(8,128)(2,1)S(1)}, bf16[192,2048]{1,0:T(8,128)(2,1)S(1)}, u32[]{:S(2)}, u32[]{:S(2)}) collective-permute-start(bf16[192,2048]{1,0:T(8,128)(2,1)S(1)} %constant_dynamic-update-slice_fusion.piece), channel_id=1, source_target_pairs={{0,8},{8,0},{16,24},{24,16},{1,9},{9,1},{17,25},{25,17},{2,10},{10... | collective-permute-start | bytes 2359304 | tf_op jit(solution)/shard_map/ppermute | solution.py:309
  20.6 10.0 %collective-permute-start.12 = (bf16[192,2048]{1,0:T(8,128)(2,1)S(1)}, bf16[192,2048]{1,0:T(8,128)(2,1)S(1)}, u32[]{:S(2)}, u32[]{:S(2)}) collective-permute-start(bf16[192,2048]{1,0:T(8,128)(2,1)S(1)} %constant_dynamic-update-slice_fusion.piece), channel_id=1, source_target_pairs={{8,16},{16,8},{9,17},{17,9},{10,18},{18,10},{11,19},{19,11},{12,20... | collective-permute-start | bytes 2359304 | tf_op jit(solution)/shard_map/ppermute | solution.py:309
  30.6 29.0 %collective-permute-start.13 = (bf16[192,2048]{1,0:T(8,128)(2,1)S(1)}, bf16[192,2048]{1,0:T(8,128)(2,1)S(1)}, u32[]{:S(2)}, u32[]{:S(2)}) collective-permute-start(bf16[192,2048]{1,0:T(8,128)(2,1)S(1)} %collective-permute-done.12.refs_1_), channel_id=1, source_target_pairs={{8,0},{16,24},{9,1},{17,25},{10,2},{18,26},{11,3},{19,27},{12,4},{... | collective-permute-start | bytes 2359304 | tf_op jit(solution)/shard_map/ppermute | solution.py:309
  36.3 30.9 %collective-permute-start.23 = (bf16[192,2048]{1,0:T(8,128)(2,1)S(1)}, bf16[192,2048]{1,0:T(8,128)(2,1)S(1)}, u32[]{:S(2)}, u32[]{:S(2)}) collective-permute-start(bf16[192,2048]{1,0:T(8,128)(2,1)S(1)} %collective-permute-done.11.refs_0_), channel_id=1, source_target_pairs={{8,16},{16,8},{9,17},{17,9},{10,18},{18,10},{11,19},{19,11},{12,20... | collective-permute-start | bytes 2359304 | tf_op jit(solution)/shard_map/ppermute | solution.py:309
  37.0 25.4 %collective-permute-start.14 = (bf16[64,2048]{1,0:T(8,128)(2,1)S(1)}, bf16[64,2048]{1,0:T(8,128)(2,1)S(1)}, u32[]{:S(2)}, u32[]{:S(2)}) collective-permute-start(bf16[64,2048]{1,0:T(8,128)(2,1)S(1)} %constant_dynamic-update-slice_fusion.4.refs_0_), channel_id=1, source_target_pairs={{0,8},{8,0},{16,24},{24,16},{1,9},{9,1},{17,25},{25,17},{2,10},{10... | collective-permute-start | bytes 786440 | tf_op jit(solution)/shard_map/ppermute | solution.py:309
  50.2 18.3 %collective-permute-start.10 = (s16[64,2176]{1,0:T(8,128)(2,1)S(1)}, s16[64,2176]{1,0:T(8,128)(2,1)S(1)}, u32[]{:S(2)}, u32[]{:S(2)}) collective-permute-start(s16[64,2176]{1,0:T(8,128)(2,1)S(1)} %get-tuple-element.57), channel_id=1, source_target_pairs={{0,6},{1,7},{2,4},{3,5},{4,2},{5,3},{6,0},{7,1},{8,14},{9,15},{10,... | collective-permute-start | bytes 835592 | tf_op jit(solution)/shard_map/ppermute | solution.py:263
  51.8 16.9 %collective-permute-start.8 = (s16[64,2176]{1,0:T(8,128)(2,1)S(1)}, s16[64,2176]{1,0:T(8,128)(2,1)S(1)}, u32[]{:S(2)}, u32[]{:S(2)}) collective-permute-start(s16[64,2176]{1,0:T(8,128)(2,1)S(1)} %get-tuple-element.55), channel_id=1, source_target_pairs={{0,2},{1,3},{2,0},{3,1},{4,6},{5,7},{6,4},{7,5},{8,10},{9,11},{10,... | collective-permute-start | bytes 835592 | tf_op jit(solution)/shard_map/ppermute | solution.py:263
  59.6 10.9 %collective-permute-start.9 = (s16[64,2176]{1,0:T(8,128)(2,1)S(1)}, s16[64,2176]{1,0:T(8,128)(2,1)S(1)}, u32[]{:S(2)}, u32[]{:S(2)}) collective-permute-start(s16[64,2176]{1,0:T(8,128)(2,1)S(1)} %get-tuple-element.56), channel_id=1, source_target_pairs={{0,4},{1,5},{2,6},{3,7},{4,0},{5,1},{6,2},{7,3},{8,12},{9,13},{10,... | collective-permute-start | bytes 835592 | tf_op jit(solution)/shard_map/ppermute | solution.py:263
  65.9 11.1 %collective-permute-start.19 = (bf16[64,2048]{1,0:T(8,128)(2,1)S(1)}, bf16[64,2048]{1,0:T(8,128)(2,1)S(1)}, u32[]{:S(2)}, u32[]{:S(2)}) collective-permute-start(bf16[64,2048]{1,0:T(8,128)(2,1)S(1)} %collective-permute-done.18.refs_3_), channel_id=1, source_target_pairs={{8,0},{16,24},{9,1},{17,25},{10,2},{18,26},{11,3},{19,27},{12,4},{... | collective-permute-start | bytes 786440 | tf_op jit(solution)/shard_map/ppermute | solution.py:309
  67.2 24.7 %collective-permute-start.24 = (bf16[192,2048]{1,0:T(8,128)(2,1)S(1)}, bf16[192,2048]{1,0:T(8,128)(2,1)S(1)}, u32[]{:S(2)}, u32[]{:S(2)}) collective-permute-start(bf16[192,2048]{1,0:T(8,128)(2,1)S(1)} %collective-permute-done.23.refs_1_), channel_id=1, source_target_pairs={{8,0},{16,24},{9,1},{17,25},{10,2},{18,26},{11,3},{19,27},{12,4},{... | collective-permute-start | bytes 2359304 | tf_op jit(solution)/shard_map/ppermute | solution.py:309
  68.5 12.8 %collective-permute-start.15 = (s16[64,2176]{1,0:T(8,128)(2,1)S(1)}, s16[64,2176]{1,0:T(8,128)(2,1)S(1)}, u32[]{:S(2)}, u32[]{:S(2)}) collective-permute-start(s16[64,2176]{1,0:T(8,128)(2,1)S(1)} %get-tuple-element.63), channel_id=1, source_target_pairs={{0,2},{1,3},{2,0},{3,1},{4,6},{5,7},{6,4},{7,5},{8,10},{9,11},{10,... | collective-permute-start | bytes 835592 | tf_op jit(solution)/shard_map/ppermute | solution.py:263
  68.6 12.7 %collective-permute-start.16 = (s16[64,2176]{1,0:T(8,128)(2,1)S(1)}, s16[64,2176]{1,0:T(8,128)(2,1)S(1)}, u32[]{:S(2)}, u32[]{:S(2)}) collective-permute-start(s16[64,2176]{1,0:T(8,128)(2,1)S(1)} %get-tuple-element.64), channel_id=1, source_target_pairs={{0,4},{1,5},{2,6},{3,7},{4,0},{5,1},{6,2},{7,3},{8,12},{9,13},{10,... | collective-permute-start | bytes 835592 | tf_op jit(solution)/shard_map/ppermute | solution.py:263
  70.5 11.7 %collective-permute-start.17 = (s16[64,2176]{1,0:T(8,128)(2,1)S(1)}, s16[64,2176]{1,0:T(8,128)(2,1)S(1)}, u32[]{:S(2)}, u32[]{:S(2)}) collective-permute-start(s16[64,2176]{1,0:T(8,128)(2,1)S(1)} %get-tuple-element.65), channel_id=1, source_target_pairs={{0,6},{1,7},{2,4},{3,5},{4,2},{5,3},{6,0},{7,1},{8,14},{9,15},{10,... | collective-permute-start | bytes 835592 | tf_op jit(solution)/shard_map/ppermute | solution.py:263
  81.3 15.3 %collective-permute-start.20 = (s16[64,2176]{1,0:T(8,128)(2,1)S(1)}, s16[64,2176]{1,0:T(8,128)(2,1)S(1)}, u32[]{:S(2)}, u32[]{:S(2)}) collective-permute-start(s16[64,2176]{1,0:T(8,128)(2,1)S(1)} %get-tuple-element.68), channel_id=1, source_target_pairs={{0,2},{1,3},{2,0},{3,1},{4,6},{5,7},{6,4},{7,5},{8,10},{9,11},{10,... | collective-permute-start | bytes 835592 | tf_op jit(solution)/shard_map/ppermute | solution.py:263
  82.2 9.8 %collective-permute-start.26 = (bf16[64,2048]{1,0:T(8,128)(2,1)S(1)}, bf16[64,2048]{1,0:T(8,128)(2,1)S(1)}, u32[]{:S(2)}, u32[]{:S(2)}) collective-permute-start(bf16[64,2048]{1,0:T(8,128)(2,1)S(1)} %collective-permute-done.25.refs_3_), channel_id=1, source_target_pairs={{8,0},{16,24},{9,1},{17,25},{10,2},{18,26},{11,3},{19,27},{12,4},{... | collective-permute-start | bytes 786440 | tf_op jit(solution)/shard_map/ppermute | solution.py:309
  83.5 18.8 %collective-permute-start.21 = (s16[64,2176]{1,0:T(8,128)(2,1)S(1)}, s16[64,2176]{1,0:T(8,128)(2,1)S(1)}, u32[]{:S(2)}, u32[]{:S(2)}) collective-permute-start(s16[64,2176]{1,0:T(8,128)(2,1)S(1)} %get-tuple-element.69), channel_id=1, source_target_pairs={{0,4},{1,5},{2,6},{3,7},{4,0},{5,1},{6,2},{7,3},{8,12},{9,13},{10,... | collective-permute-start | bytes 835592 | tf_op jit(solution)/shard_map/ppermute | solution.py:263
  85.5 16.8 %collective-permute-start.22 = (s16[64,2176]{1,0:T(8,128)(2,1)S(1)}, s16[64,2176]{1,0:T(8,128)(2,1)S(1)}, u32[]{:S(2)}, u32[]{:S(2)}) collective-permute-start(s16[64,2176]{1,0:T(8,128)(2,1)S(1)} %get-tuple-element.70), channel_id=1, source_target_pairs={{0,6},{1,7},{2,4},{3,5},{4,2},{5,3},{6,0},{7,1},{8,14},{9,15},{10,... | collective-permute-start | bytes 835592 | tf_op jit(solution)/shard_map/ppermute | solution.py:263
  96.3 9.5 %collective-permute-start.28 = (s16[64,2176]{1,0:T(8,128)(2,1)S(1)}, s16[64,2176]{1,0:T(8,128)(2,1)S(1)}, u32[]{:S(2)}, u32[]{:S(2)}) collective-permute-start(s16[64,2176]{1,0:T(8,128)(2,1)S(1)} %get-tuple-element.79), channel_id=1, source_target_pairs={{0,4},{1,5},{2,6},{3,7},{4,0},{5,1},{6,2},{7,3},{8,12},{9,13},{10,... | collective-permute-start | bytes 835592 | tf_op jit(solution)/shard_map/ppermute | solution.py:263
  96.5 9.3 %collective-permute-start.29 = (s16[64,2176]{1,0:T(8,128)(2,1)S(1)}, s16[64,2176]{1,0:T(8,128)(2,1)S(1)}, u32[]{:S(2)}, u32[]{:S(2)}) collective-permute-start(s16[64,2176]{1,0:T(8,128)(2,1)S(1)} %get-tuple-element.80), channel_id=1, source_target_pairs={{0,6},{1,7},{2,4},{3,5},{4,2},{5,3},{6,0},{7,1},{8,14},{9,15},{10,... | collective-permute-start | bytes 835592 | tf_op jit(solution)/shard_map/ppermute | solution.py:263
  (8 other events, 42.7 us)
